TPU v7x, 512 devices: a whole 4x4x16 slice. The times are simulated.
512 devices in a mesh: ctx: 128 (over y, z, core), head: 4 (over x).
Axes of the slice: x: 4, y: 4, z: 16, core: 2. Of those that a mesh axis runs over, the one named last changes fastest.
Arguments:
- branch_q: bfloat16 [16384, 4, 1024], P('ctx', 'head'), may hold values from -6 to 6
- branch_k: bfloat16 [16384, 4, 128], P('ctx', 'head'), may hold values from -6 to 6
- branch_v: bfloat16 [16384, 4, 128], P('ctx', 'head'), may hold values from -6 to 6
- branch_o: bfloat16 [16384, 4, 1024], P('ctx', 'head'), may hold values from -4 to 4
- branch_dout: bfloat16 [16384, 4, 1024], P('ctx', 'head'), may hold values from -512 to 512
- prompt_q: bfloat16 [256, 4, 1024], P('ctx', 'head'), may hold values from -6 to 6
- prompt_k: bfloat16 [256, 4, 128], P('ctx', 'head'), may hold values from -6 to 6
- prompt_v: bfloat16 [256, 4, 128], P('ctx', 'head'), may hold values from -6 to 6
- prompt_o: bfloat16 [256, 4, 1024], P('ctx', 'head'), may hold values from -4 to 4
- prompt_dout: bfloat16 [256, 4, 1024], P('ctx', 'head'), may hold values from -512 to 512
- gains: float32 [2, 128], replicated, may hold values from 0.8 to 2
- parents: int32 [128], P('ctx'), may hold values from 0 to 128, as said below
- depth: int32 [16384], P('ctx'), may hold values from 128 to 1279, as said below
Outputs:
- branch_dq: bfloat16 [16384, 4, 1024], P('ctx', 'head')
- branch_dk: bfloat16 [16384, 4, 128], P('ctx', 'head')
- branch_dv: bfloat16 [16384, 4, 128], P('ctx', 'head')
- prompt_dq: bfloat16 [256, 4, 1024], P('ctx', 'head')
- prompt_dk: bfloat16 [256, 4, 128], P('ctx', 'head')
- prompt_dv: bfloat16 [256, 4, 128], P('ctx', 'head')
- gain_grads: float32 [2, 128], replicated
Inputs may be any that keep to these rules, and one draw needn't show every extreme that they name: `parents`: the parent of a branch block is a prompt block or an earlier branch block of the same subtree. A subtree is a run of consecutive branch blocks whose first block's parent is a prompt block; a run has at most 8 blocks, and some run has exactly 8. depth of a branch token = 128 times the number of its block's proper ancestor blocks, prompt blocks up to the fork included, plus its offset in its block.
All inputs are finite; a program needn't handle non-finite values.
Results may differ from a plain program's by a relative error of at most 0.0093.
Values may be sent and summed in bfloat16 or wider, within the bound.
A program may use at most 64 MiB of HBM per device.

v0:
```python
import jax
import jax.numpy as jnp
from jax import lax
from jax.sharding import PartitionSpec as P

BLK = 128
SUB = 8
PFX = 256


EPS = 1e-06
THETA = 1000000.0


def shifted(value, axis, steps):
    count = lax.axis_size(axis)
    leading, last = (max(0, -steps), min(count, count - steps))
    return lax.ppermute(value, axis, [(source, source + steps) for source in range(leading, last)])


def angles(positions, head_size):
    half_size = head_size // 2
    frequencies = THETA ** (-(jnp.arange(half_size, dtype=jnp.float32) * 2.0) / head_size)
    return positions.astype(jnp.float32)[:, None] * frequencies[None, :]


def rotate(values, angle_table):
    half_size = values.shape[-1] // 2
    cosine = jnp.cos(angle_table)
    sine_part = jnp.sin(angle_table)
    first_half = values[..., :half_size]
    second_half = values[..., half_size:]
    return jnp.concatenate(
        [
            first_half * cosine - second_half * sine_part,
            second_half * cosine + first_half * sine_part,
        ],
        axis=-1,
    )


def prepare(raw_values, gain_vector, angle_table):
    widened = raw_values.astype(jnp.float32)
    inverse = lax.rsqrt(jnp.mean(widened * widened, axis=-1, keepdims=True) + EPS)
    unit_values = widened * inverse
    rotated = rotate(unit_values * gain_vector, angle_table).astype(jnp.bfloat16)
    return (unit_values, inverse, rotated)


def norm_back(grad_rotated, unit_values, inverse, gain_vector, angle_table):
    grad_normed = rotate(grad_rotated, -angle_table)
    scaled = grad_normed * gain_vector
    grad_raw = (
        scaled - unit_values * jnp.mean(scaled * unit_values, axis=-1, keepdims=True)
    ) * inverse
    gain_part = jnp.sum((grad_normed * unit_values).reshape(-1, unit_values.shape[-1]), axis=0)
    return (grad_raw, gain_part)


def per_device(
    branch_q,
    branch_k,
    branch_v,
    branch_o,
    branch_dout,
    prompt_q,
    prompt_k,
    prompt_v,
    prompt_o,
    prompt_dout,
    gains,
    parents,
    depth,
):
    head_size = branch_k.shape[-1]
    tok_local = branch_k.shape[0]
    prompt_local = prompt_k.shape[0]
    group_size = branch_q.shape[-1] // head_size
    blocks_local = tok_local // BLK
    reach_back = (SUB + blocks_local - 2) // blocks_local
    prompt_blocks = PFX // BLK
    piece_size = 2 * BLK
    score_scale = head_size ** (-0.5)
    device = lax.axis_index("ctx")
    gain_q = gains[0]
    gain_k = gains[1]
    row_count = tok_local + prompt_local
    angle_branch = angles(depth, head_size)
    angle_prompt = angles(
        device * prompt_local + jnp.arange(prompt_local, dtype=jnp.int32), head_size
    )
    angle_rows = jnp.concatenate([angle_branch, angle_prompt])[:, None, :]
    queries = jnp.concatenate([branch_q[:, 0], prompt_q[:, 0]]).reshape(
        row_count, group_size, head_size
    )
    unit_q, inverse_q, rotated_q = prepare(queries, gain_q, angle_rows)
    unit_bk, inverse_bk, rotated_bk = prepare(branch_k[:, 0], gain_k, angle_branch)
    unit_pk, inverse_pk, rotated_pk = prepare(prompt_k[:, 0], gain_k, angle_prompt)
    value_local = branch_v[:, 0]
    prompt_keys, prompt_values = (
        lax.all_gather(rotated_pk, "ctx", axis=0, tiled=True),
        lax.all_gather(prompt_v[:, 0], "ctx", axis=0, tiled=True),
    )
    fetched = [(rotated_bk, value_local, parents)]
    for distance in range(1, reach_back + 1):
        fetched.insert(0, shifted((rotated_bk, value_local, parents), "ctx", distance))
    window_k = jnp.stack([member[0] for member in fetched])
    window_v = jnp.stack([member[1] for member in fetched])
    window_parents = jnp.stack([member[2] for member in fetched])
    window_blocks = (reach_back + 1) * blocks_local
    flat_parents = window_parents.reshape(window_blocks)
    first_block = (device - reach_back) * blocks_local
    slot_ids = jnp.arange(window_blocks, dtype=jnp.int32)

    def climb(step_index, climb_state):
        current, ancestors, fork_blocks = climb_state
        branchy = current >= prompt_blocks
        located = current - prompt_blocks - first_block
        matched = (slot_ids[None, :] == located[:, None]) & branchy[:, None]
        upward = jnp.sum(jnp.where(matched, flat_parents[None, :], 0), axis=1).astype(jnp.int32)
        return (
            jnp.where(branchy, upward, current),
            ancestors | matched,
            jnp.where(branchy, fork_blocks, current),
        )

    start_state = (
        device * blocks_local + jnp.arange(blocks_local, dtype=jnp.int32) + prompt_blocks,
        jnp.zeros((blocks_local, window_blocks), dtype=bool),
        jnp.zeros((blocks_local,), jnp.int32),
    )
    unused, ancestors, fork_blocks = lax.fori_loop(0, SUB + 1, climb, start_state)
    offsets = jnp.arange(BLK, dtype=jnp.int32)
    branch_limit = jnp.broadcast_to(
        (BLK * (fork_blocks + 1))[:, None], (blocks_local, BLK)
    ).reshape(tok_local)
    prompt_limit = device * prompt_local + jnp.arange(prompt_local, dtype=jnp.int32) + 1
    row_limit = jnp.concatenate([branch_limit, prompt_limit])
    branch_seen = jnp.broadcast_to(
        ancestors[:, None, :], (blocks_local, BLK, window_blocks)
    ).reshape(tok_local, window_blocks)
    row_seen = jnp.concatenate([branch_seen, jnp.zeros((prompt_local, window_blocks), dtype=bool)])
    branch_own = jnp.broadcast_to(
        (reach_back * blocks_local + jnp.arange(blocks_local, dtype=jnp.int32))[:, None],
        (blocks_local, BLK),
    ).reshape(tok_local)
    row_own = jnp.concatenate([branch_own, jnp.full((prompt_local,), -1, jnp.int32)])
    row_offset = jnp.concatenate(
        [jnp.tile(offsets, blocks_local), jnp.zeros((prompt_local,), jnp.int32)]
    )

    def piece_mask(key_start):
        key_ids = key_start + jnp.arange(piece_size, dtype=jnp.int32)
        prompt_key = key_ids < PFX
        window_pos = key_ids - PFX
        key_block = window_pos // BLK
        key_offset = window_pos % BLK
        prompt_ok = prompt_key[None, :] & (key_ids[None, :] < row_limit[:, None])
        block_seen = jnp.any(
            row_seen[:, :, None] & (key_block[None, None, :] == slot_ids[None, :, None]), axis=1
        )
        causal = (key_block[None, :] != row_own[:, None]) | (
            key_offset[None, :] <= row_offset[:, None]
        )
        return prompt_ok | jnp.logical_not(prompt_key)[None, :] & block_seen & causal

    key_total = PFX + window_blocks * BLK
    piece_count = key_total // piece_size
    all_keys = jnp.concatenate([prompt_keys, window_k.reshape(-1, head_size)]).reshape(
        piece_count, piece_size, head_size
    )
    all_values = jnp.concatenate([prompt_values, window_v.reshape(-1, head_size)]).reshape(
        piece_count, piece_size, head_size
    )
    key_starts = jnp.arange(piece_count, dtype=jnp.int32) * piece_size
    query_rows = rotated_q.reshape(row_count * group_size, head_size)
    grad_rows = jnp.concatenate([branch_dout[:, 0], prompt_dout[:, 0]]).reshape(
        row_count * group_size, head_size
    )
    out_rows = jnp.concatenate([branch_o[:, 0], prompt_o[:, 0]]).reshape(
        row_count * group_size, head_size
    )
    row_delta = jnp.sum(
        grad_rows.astype(jnp.float32) * out_rows.astype(jnp.float32), axis=-1
    ).reshape(row_count, group_size)

    def scores_of(key_piece):
        products = jnp.einsum(
            "qd,kd->qk", query_rows, key_piece, preferred_element_type=jnp.float32
        )
        return products.reshape(row_count, group_size, piece_size) * score_scale

    def add_total(running, scan_item):
        key_start, key_piece = scan_item
        visible = piece_mask(key_start)[:, None, :]
        return (
            running + jnp.sum(jnp.where(visible, jnp.exp(scores_of(key_piece)), 0.0), axis=-1),
            None,
        )

    totals, unused_rows = lax.scan(
        add_total, jnp.zeros((row_count, group_size), jnp.float32), (key_starts, all_keys)
    )
    log_total = jnp.log(totals)

    def back_piece(grad_q, scan_item):
        key_start, key_piece, value_piece = scan_item
        visible = piece_mask(key_start)[:, None, :]
        weights = jnp.where(visible, jnp.exp(scores_of(key_piece) - log_total[:, :, None]), 0.0)
        weight_half = weights.astype(jnp.bfloat16).reshape(row_count * group_size, piece_size)
        grad_v = jnp.einsum("qk,qd->kd", weight_half, grad_rows, preferred_element_type=jnp.float32)
        grad_p = jnp.einsum(
            "qd,kd->qk", grad_rows, value_piece, preferred_element_type=jnp.float32
        ).reshape(row_count, group_size, piece_size)
        grad_s = (
            (weights * (grad_p - row_delta[:, :, None]))
            .astype(jnp.bfloat16)
            .reshape(row_count * group_size, piece_size)
        )
        grad_k = (
            jnp.einsum("qk,qd->kd", grad_s, query_rows, preferred_element_type=jnp.float32)
            * score_scale
        )
        added = grad_q + jnp.einsum(
            "qk,kd->qd", grad_s, key_piece, preferred_element_type=jnp.float32
        )
        return (added, (grad_k, grad_v))

    grad_q, piece_grads = lax.scan(
        back_piece,
        jnp.zeros((row_count * group_size, head_size), jnp.float32),
        (key_starts, all_keys, all_values),
    )
    grad_keys = piece_grads[0].reshape(key_total, head_size)
    grad_values = piece_grads[1].reshape(key_total, head_size)
    prompt_gk, prompt_gv = (
        lax.psum_scatter(grad_keys[:PFX], "ctx", scatter_dimension=0, tiled=True),
        lax.psum_scatter(grad_values[:PFX], "ctx", scatter_dimension=0, tiled=True),
    )
    window_gk = grad_keys[PFX:].reshape(reach_back + 1, tok_local, head_size)
    window_gv = grad_values[PFX:].reshape(reach_back + 1, tok_local, head_size)
    total_k = window_gk[reach_back]
    total_v = window_gv[reach_back]
    for distance in range(1, reach_back + 1):
        back_k, back_v = (
            shifted(window_gk[reach_back - distance].astype(jnp.bfloat16), "ctx", -distance).astype(
                jnp.float32
            ),
            shifted(window_gv[reach_back - distance].astype(jnp.bfloat16), "ctx", -distance).astype(
                jnp.float32
            ),
        )
        total_k = total_k + back_k
        total_v = total_v + back_v
    grad_all_q = (grad_q * score_scale).reshape(row_count, group_size, head_size)
    raw_q, gain_part_q = norm_back(grad_all_q, unit_q, inverse_q, gain_q, angle_rows)
    raw_bk, gain_bk = norm_back(total_k, unit_bk, inverse_bk, gain_k, angle_branch)
    raw_pk, gain_pk = norm_back(prompt_gk, unit_pk, inverse_pk, gain_k, angle_prompt)
    sum_q, sum_k = lax.psum((gain_part_q, gain_bk + gain_pk), ("ctx", "head"))
    token_total = (tok_local + prompt_local) * lax.axis_size("ctx")
    head_total = lax.axis_size("head")
    factor_q = (token_total * head_total * group_size) ** (-0.5)
    factor_k = (token_total * head_total) ** (-0.5)
    gain_grads = jnp.stack([sum_q * factor_q, sum_k * factor_k])
    branch_dq = raw_q[:tok_local].reshape(tok_local, 1, group_size * head_size).astype(jnp.bfloat16)
    prompt_dq = (
        raw_q[tok_local:].reshape(prompt_local, 1, group_size * head_size).astype(jnp.bfloat16)
    )
    return (
        branch_dq,
        raw_bk[:, None].astype(jnp.bfloat16),
        total_v[:, None].astype(jnp.bfloat16),
        prompt_dq,
        raw_pk[:, None].astype(jnp.bfloat16),
        prompt_gv[:, None].astype(jnp.bfloat16),
        gain_grads,
    )


def solution(mesh):
    return jax.shard_map(
        per_device,
        mesh=mesh,
        in_specs=(
            P("ctx", "head", None),
            P("ctx", "head", None),
            P("ctx", "head", None),
            P("ctx", "head", None),
            P("ctx", "head", None),
            P("ctx", "head", None),
            P("ctx", "head", None),
            P("ctx", "head", None),
            P("ctx", "head", None),
            P("ctx", "head", None),
            P(),
            P("ctx"),
            P("ctx"),
        ),
        out_specs=(
            P("ctx", "head", None),
            P("ctx", "head", None),
            P("ctx", "head", None),
            P("ctx", "head", None),
            P("ctx", "head", None),
            P("ctx", "head", None),
            P(),
        ),
        check_vma=False,
    )
```

profile of v0, /device:TPU:1, one launch (start us, length us, event | category | flops | bytes accessed | tf_op | source)
XLA Modules:
  0.0 1014.4 jit_solution(6834789810668962888)
XLA Ops:
  10.8 10.2 %collective-permute-start.7 = (bf16[128,128]{1,0:T(8,128)(2,1)S(1)}, bf16[128,128]{1,0:T(8,128)(2,1)S(1)}, u32[]{:S(2)}, u32[]{:S(2)}) collective-permute-start(bf16[128,128]{1,0:T(8,128)(2,1)S(1)} %pad_maximum_fusion.8), channel_id=1, source_target_pairs={{0,28},{4,32},{8,36},{12,40},{16,44},{20,48},{24,52},{28,56},{32,6... | collective-permute-start | bytes 98312 | tf_op jit(solution)/shard_map/ppermute | solution.py:18
  21.0 6.3 collective-permute-start.8
  27.3 5.2 collective-permute-start.9
  32.5 3.1 collective-permute-start.10
  35.6 5.1 collective-permute-start
  43.2 72.9 %all-gather.1 = bf16[128,2,128]{2,1,0:T(2,128)(2,1)S(1)} all-gather(bf16[1,2,128]{2,1,0:T(2,128)(2,1)S(1)} %maximum_bitcast_fusion), channel_id=1, replica_groups=mesh['ctx'=128,'head'=4] {'ctx'}, dimensions={0}, use_global_device_ids=true | all-gather | bytes 66048 | tf_op jit(solution)/shard_map/all_gather | solution.py:101
  117.5 81.3 %all-gather = bf16[256,1,128]{2,1,0:T(2,128)(2,1)S(1)} all-gather(bf16[2,1,128]{2,1,0:T(2,128)(2,1)S(1)} %copy.30), channel_id=2, replica_groups=mesh['ctx'=128,'head'=4] {'ctx'}, dimensions={0}, use_global_device_ids=true | all-gather | bytes 66048 | tf_op jit(solution)/shard_map/all_gather | solution.py:102
  199.1 1.1 negate_cosine_fusion
  201.2 1.3 dynamic-slice
  203.2 3.9 collective-permute-start.1
  207.4 7.1 collective-permute-start.2
  214.8 4.9 collective-permute-start.3
  220.1 8.2 collective-permute-start.4
  228.6 3.1 collective-permute-start.5
  231.9 5.7 collective-permute-start.6
  238.5 5.8 collective-permute-start.11
  244.3 4.6 stack.93
  248.8 12.0 %while.48 = (s32[]{:T(128)}, s32[1]{0:T(128)}, pred[1,8]{1,0:T(4,128)(4,1)S(1)}, s32[1]{0:T(128)}, s32[]{:T(128)}, /*index=5*/s32[8,1]{0,1:T(1,128)S(1)}, s32[]{:T(128)}, s32[1]{0:T(128)}, s32[1]{0:T(128)}, s32[]{:T(128)}) while((s32[]{:T(128)}, s32[1]{0:T(128)}, pred[1,8]{1,0:T(4,128)(4,1)S(1)}, s32[1]{0:T(128)}, s32[]{:T(128)}, ...), condition=%wide.region_4.0_spmd.clone, body=%wide.region_2.4_spmd.clone.sunk | while | flops 71 | bytes 240 | solution.py:132
  260.9 5.7 collective-permute-start.12
  266.6 3.7 collective-permute-start.13
  270.3 4.0 collective-permute-start.14
  274.3 5.8 collective-permute-start.15
  280.1 5.7 collective-permute-start.16
  285.8 1.9 collective-permute-start.17
  287.8 9.6 collective-permute-start.18
  297.5 18.9 %while.49 = (s32[]{:T(128)}, f32[130,8]{1,0:T(8,128)S(1)}, s32[5]{0:T(128)S(1)}, s32[130]{0:T(256)S(1)}, pred[130,8]{1,0:T(8,128)(4,1)S(1)}, /*index=5*/bf16[5,2...) while((s32[]{:T(128)}, f32[130,8]{1,0:T(8,128)S(1)}, ...), condition=%wide.region_9.10_spmd.clone, body=%wide.region_6.0_spmd.clone.sunk | while | flops 69731088 | bytes 506427 | solution.py:201
  316.4 2.0 collective-permute-start.19
  318.4 2.9 collective-permute-start.20
  323.1 35.6 %while.50 = (s32[]{:T(128)}, f32[1040,128]{1,0:T(8,128)S(1)}, f32[5,256,128]{2,1,0:T(8,128)}, f32[5,256,128]{2,1,0:T(8,128)}, s32[5]{0:T(128)S(1)}, /*index=5*/s...) while((s32[]{:T(128)}, f32[1040,128]{1,0:T(8,128)S(1)}, ...), condition=%wide.wide.region_13.14_spmd.clone, body=%wide.wide.region_11.13_spmd.clone.sunk | while | flops 343723776 | bytes 7544631 | solution.py:229
  326.7 1.2 fusion.176
  327.8 1.0 fusion.177
  333.8 1.2 fusion.176
  335.0 1.0 fusion.177
  336.3 1.0 fusion.178
  340.9 1.2 fusion.176
  343.4 1.0 fusion.178
  348.0 1.2 fusion.176
  349.2 1.0 fusion.177
  350.5 1.0 fusion.178
  355.1 1.2 fusion.176
  356.3 1.0 fusion.177
  358.7 1.6 slice_bitcast_fusion.1
  360.3 1.1 slice.143
  361.3 1.1 slice.154
  363.4 1.9 collective-permute-start.21
  365.4 1.3 collective-permute-start.22
  366.7 1.3 collective-permute-start.23
  368.0 1.3 collective-permute-start.24
  369.3 1.3 collective-permute-start.25
  372.8 485.7 %all-reduce.9 = bf16[256,128]{1,0:T(8,128)(2,1)S(1)} all-reduce(f32[256,128]{1,0:T(8,128)S(1)} %slice_bitcast_fusion), channel_id=4, replica_groups=mesh['ctx'=128,'head'=4] {'ctx'}, use_global_device_ids=true, to_apply=%region_18.19.clone | all-reduce | flops 32768 | bytes 196608
  858.5 1.3 collective-permute-start.26
  859.8 1.3 collective-permute-start.27
  863.1 7.5 collective-permute-start.28
  870.7 1.3 collective-permute-start.29
  872.0 1.3 collective-permute-start.30
  873.3 1.3 collective-permute-start.31
  874.6 1.3 collective-permute-start.32
  876.5 1.3 collective-permute-start.33
  877.8 1.3 collective-permute-start.34
  879.1 1.7 collective-permute-done.31
  880.8 4.1 collective-permute-done.32
  884.9 2.7 collective-permute-done.33
  887.6 5.2 collective-permute-done.34
  895.2 111.2 %all-reduce.4 = (f32[128]{0:T(128)S(1)}, f32[128]{0:T(128)S(1)}) all-reduce(f32[128]{0:T(128)S(1)} %add.378, f32[128]{0:T(128)S(1)} %get-tuple-element.496), channel_id=1, replica_groups=mesh['ctx'=128,'head'=4] {'ctx','head'}, use_global_device_ids=true, to_apply=%region_23.24 | all-reduce | flops 256 | bytes 2048 | tf_op jit(solution)/shard_map/psum | solution.py:259
  (263 shorter events, 67.9 us)
Async XLA Ops:
  7.2 110.0 %copy-start.11 = (bf16[2,1,1024]{2,0,1:T(2,128)(2,1)S(1)}, bf16[2,1,1024]{2,0,1:T(2,128)(2,1)}, u32[]{:S(2)}) copy-start(bf16[2,1,1024]{2,0,1:T(2,128)(2,1)} %param.24) | copy-start | bytes 12292
  7.2 110.3 %copy-start.12 = (bf16[2,1,128]{2,0,1:T(2,128)(2,1)S(1)}, bf16[2,1,128]{2,0,1:T(2,128)(2,1)}, u32[]{:S(2)}) copy-start(bf16[2,1,128]{2,0,1:T(2,128)(2,1)} %param.26) | copy-start | bytes 1540
  7.2 191.6 %copy-start.4 = (bf16[128,1,1024]{2,0,1:T(8,128)(2,1)S(1)}, bf16[128,1,1024]{2,0,1:T(8,128)(2,1)}, u32[]{:S(2)}) copy-start(bf16[128,1,1024]{2,0,1:T(8,128)(2,1)} %param.23) | copy-start | bytes 786436
  7.2 191.6 %copy-start.9 = (bf16[2,1,1024]{2,0,1:T(2,128)(2,1)S(1)}, bf16[2,1,1024]{2,0,1:T(2,128)(2,1)}, u32[]{:S(2)}) copy-start(bf16[2,1,1024]{2,0,1:T(2,128)(2,1)} %param.28) | copy-start | bytes 12292
  7.2 887.0 %all-reduce.8.cloned.1.call-start = ((), (), s32[]{:S(2)}) async-start(), calls=%async_computation | async-start | bytes 262144
  10.8 250.1 %collective-permute-start.7 = (bf16[128,128]{1,0:T(8,128)(2,1)S(1)}, bf16[128,128]{1,0:T(8,128)(2,1)S(1)}, u32[]{:S(2)}, u32[]{:S(2)}) collective-permute-start(bf16[128,128]{1,0:T(8,128)(2,1)S(1)} %pad_maximum_fusion.8), channel_id=1, source_target_pairs={{0,28},{4,32},{8,36},{12,40},{16,44},{20,48},{24,52},{28,56},{32,6... | collective-permute-start | bytes 98312 | tf_op jit(solution)/shard_map/ppermute | solution.py:18
  21.0 245.6 %collective-permute-start.8 = (bf16[128,128]{1,0:T(8,128)(2,1)S(1)}, bf16[128,128]{1,0:T(8,128)(2,1)S(1)}, u32[]{:S(2)}, u32[]{:S(2)}) collective-permute-start(bf16[128,128]{1,0:T(8,128)(2,1)S(1)} %pad_maximum_fusion.8), channel_id=1, source_target_pairs={{0,24},{4,28},{8,32},{12,36},{16,40},{20,44},{24,48},{28,52},{32,5... | collective-permute-start | bytes 98312 | tf_op jit(solution)/shard_map/ppermute | solution.py:18
  27.3 243.0 %collective-permute-start.9 = (bf16[128,128]{1,0:T(8,128)(2,1)S(1)}, bf16[128,128]{1,0:T(8,128)(2,1)S(1)}, u32[]{:S(2)}, u32[]{:S(2)}) collective-permute-start(bf16[128,128]{1,0:T(8,128)(2,1)S(1)} %pad_maximum_fusion.8), channel_id=1, source_target_pairs={{0,20},{4,24},{8,28},{12,32},{16,36},{20,40},{24,44},{28,48},{32,5... | collective-permute-start | bytes 98312 | tf_op jit(solution)/shard_map/ppermute | solution.py:18
  32.5 241.8 %collective-permute-start.10 = (bf16[128,128]{1,0:T(8,128)(2,1)S(1)}, bf16[128,128]{1,0:T(8,128)(2,1)S(1)}, u32[]{:S(2)}, u32[]{:S(2)}) collective-permute-start(bf16[128,128]{1,0:T(8,128)(2,1)S(1)} %pad_maximum_fusion.8), channel_id=1, source_target_pairs={{0,16},{4,20},{8,24},{12,28},{16,32},{20,36},{24,40},{28,44},{32,4... | collective-permute-start | bytes 98312 | tf_op jit(solution)/shard_map/ppermute | solution.py:18
  35.6 167.6 %collective-permute-start = (s32[1]{0:T(128)}, s32[1]{0:T(128)}, u32[]{:S(2)}, u32[]{:S(2)}) collective-permute-start(s32[1]{0:T(128)} %param.30), channel_id=1, source_target_pairs={{0,28},{4,32},{8,36},{12,40},{16,44},{20,48},{24,52},{28,56},{32,6... | collective-permute-start | bytes 20 | tf_op jit(solution)/shard_map/ppermute | solution.py:18
  117.2 81.8 %copy-start.3 = (bf16[128,1,1024]{2,0,1:T(8,128)(2,1)S(1)}, bf16[128,1,1024]{2,0,1:T(8,128)(2,1)}, u32[]{:S(2)}) copy-start(bf16[128,1,1024]{2,0,1:T(8,128)(2,1)} %param.22) | copy-start | bytes 786436
  117.2 81.8 %copy-start.10 = (bf16[2,1,1024]{2,0,1:T(2,128)(2,1)S(1)}, bf16[2,1,1024]{2,0,1:T(2,128)(2,1)}, u32[]{:S(2)}) copy-start(bf16[2,1,1024]{2,0,1:T(2,128)(2,1)} %param.27) | copy-start | bytes 12292
  200.7 69.6 %copy-start.7 = (bf16[128,1,128]{2,0,1:T(8,128)(2,1)S(1)}, bf16[128,1,128]{2,0,1:T(8,128)(2,1)}, u32[]{:S(2)}) copy-start(bf16[128,1,128]{2,0,1:T(8,128)(2,1)} %param.21) | copy-start | bytes 98308
  200.9 96.6 %copy-start.5 = (s32[130]{0:T(256)S(1)}, s32[130]{0:T(256)}, u32[]{:S(2)}) copy-start(s32[130]{0:T(256)} %constant.212.clone.2) | copy-start | bytes 1564
  200.9 96.6 %copy-start.6 = (s32[130]{0:T(256)S(1)}, s32[130]{0:T(256)}, u32[]{:S(2)}) copy-start(s32[130]{0:T(256)} %constant.214.clone.2) | copy-start | bytes 1564
  203.2 4.2 collective-permute-start.1
  207.4 7.4 collective-permute-start.2
  214.8 5.3 collective-permute-start.3
  220.1 8.5 collective-permute-start.4
  228.6 3.4 collective-permute-start.5
  231.9 6.5 collective-permute-start.6
  238.5 41.7 %collective-permute-start.11 = (bf16[128,128]{1,0:T(8,128)(2,1)S(1)}, bf16[128,128]{1,0:T(8,128)(2,1)S(1)}, u32[]{:S(2)}, u32[]{:S(2)}) collective-permute-start(bf16[128,128]{1,0:T(8,128)(2,1)S(1)} %pad_maximum_fusion.8), channel_id=1, source_target_pairs={{0,12},{4,16},{8,20},{12,24},{16,28},{20,32},{24,36},{28,40},{32,4... | collective-permute-start | bytes 98312 | tf_op jit(solution)/shard_map/ppermute | solution.py:18
  260.9 24.9 %collective-permute-start.12 = (bf16[128,128]{1,0:T(8,128)(2,1)S(1)}, bf16[128,128]{1,0:T(8,128)(2,1)S(1)}, u32[]{:S(2)}, u32[]{:S(2)}) collective-permute-start(bf16[128,128]{1,0:T(8,128)(2,1)S(1)} %pad_maximum_fusion.8), channel_id=1, source_target_pairs={{0,8},{4,12},{8,16},{12,20},{16,24},{20,28},{24,32},{28,36},{32,40... | collective-permute-start | bytes 98312 | tf_op jit(solution)/shard_map/ppermute | solution.py:18
  266.6 21.2 %collective-permute-start.13 = (bf16[128,128]{1,0:T(8,128)(2,1)S(1)}, bf16[128,128]{1,0:T(8,128)(2,1)S(1)}, u32[]{:S(2)}, u32[]{:S(2)}) collective-permute-start(bf16[128,128]{1,0:T(8,128)(2,1)S(1)} %pad_maximum_fusion.8), channel_id=1, source_target_pairs={{0,4},{4,8},{8,12},{12,16},{16,20},{20,24},{24,28},{28,32},{32,36}... | collective-permute-start | bytes 98312 | tf_op jit(solution)/shard_map/ppermute | solution.py:18
  270.3 46.1 %collective-permute-start.14 = (bf16[128,128]{1,0:T(8,128)(2,1)S(1)}, bf16[128,128]{1,0:T(8,128)(2,1)S(1)}, u32[]{:S(2)}, u32[]{:S(2)}) collective-permute-start(bf16[128,128]{1,0:T(8,128)(2,1)S(1)} %bitcast.351), channel_id=1, source_target_pairs={{0,28},{4,32},{8,36},{12,40},{16,44},{20,48},{24,52},{28,56},{32,6... | collective-permute-start | bytes 98312 | tf_op jit(solution)/shard_map/ppermute | solution.py:18
  274.3 44.1 %collective-permute-start.15 = (bf16[128,128]{1,0:T(8,128)(2,1)S(1)}, bf16[128,128]{1,0:T(8,128)(2,1)S(1)}, u32[]{:S(2)}, u32[]{:S(2)}) collective-permute-start(bf16[128,128]{1,0:T(8,128)(2,1)S(1)} %bitcast.352), channel_id=1, source_target_pairs={{0,24},{4,28},{8,32},{12,36},{16,40},{20,44},{24,48},{28,52},{32,5... | collective-permute-start | bytes 98312 | tf_op jit(solution)/shard_map/ppermute | solution.py:18
  280.1 41.2 %collective-permute-start.16 = (bf16[128,128]{1,0:T(8,128)(2,1)S(1)}, bf16[128,128]{1,0:T(8,128)(2,1)S(1)}, u32[]{:S(2)}, u32[]{:S(2)}) collective-permute-start(bf16[128,128]{1,0:T(8,128)(2,1)S(1)} %bitcast.353), channel_id=1, source_target_pairs={{0,20},{4,24},{8,28},{12,32},{16,36},{20,40},{24,44},{28,48},{32,5... | collective-permute-start | bytes 98312 | tf_op jit(solution)/shard_map/ppermute | solution.py:18
  285.8 35.5 %collective-permute-start.17 = (bf16[128,128]{1,0:T(8,128)(2,1)S(1)}, bf16[128,128]{1,0:T(8,128)(2,1)S(1)}, u32[]{:S(2)}, u32[]{:S(2)}) collective-permute-start(bf16[128,128]{1,0:T(8,128)(2,1)S(1)} %bitcast.354), channel_id=1, source_target_pairs={{0,16},{4,20},{8,24},{12,28},{16,32},{20,36},{24,40},{28,44},{32,4... | collective-permute-start | bytes 98312 | tf_op jit(solution)/shard_map/ppermute | solution.py:18
  287.8 33.6 %collective-permute-start.18 = (bf16[128,128]{1,0:T(8,128)(2,1)S(1)}, bf16[128,128]{1,0:T(8,128)(2,1)S(1)}, u32[]{:S(2)}, u32[]{:S(2)}) collective-permute-start(bf16[128,128]{1,0:T(8,128)(2,1)S(1)} %bitcast.355), channel_id=1, source_target_pairs={{0,12},{4,16},{8,20},{12,24},{16,28},{20,32},{24,36},{28,40},{32,4... | collective-permute-start | bytes 98312 | tf_op jit(solution)/shard_map/ppermute | solution.py:18
  316.4 5.0 collective-permute-start.19
  318.4 3.9 collective-permute-start.20
  321.5 1.6 copy-start.2
  363.4 495.1 %collective-permute-start.21 = (bf16[128,128]{1,0:T(8,128)(2,1)S(1)}, bf16[128,128]{1,0:T(8,128)(2,1)S(1)}, u32[]{:S(2)}, u32[]{:S(2)}) collective-permute-start(bf16[128,128]{1,0:T(8,128)(2,1)S(1)} %get-tuple-element.575), channel_id=1, source_target_pairs={{4,0},{8,4},{12,8},{16,12},{20,16},{24,20},{28,24},{32,28},{36,32}... | collective-permute-start | bytes 98312 | tf_op jit(solution)/shard_map/ppermute | solution.py:18
  365.4 494.4 %collective-permute-start.22 = (bf16[128,128]{1,0:T(8,128)(2,1)S(1)}, bf16[128,128]{1,0:T(8,128)(2,1)S(1)}, u32[]{:S(2)}, u32[]{:S(2)}) collective-permute-start(bf16[128,128]{1,0:T(8,128)(2,1)S(1)} %get-tuple-element.581), channel_id=1, source_target_pairs={{8,0},{12,4},{16,8},{20,12},{24,16},{28,20},{32,24},{36,28},{40,32... | collective-permute-start | bytes 98312 | tf_op jit(solution)/shard_map/ppermute | solution.py:18
  366.7 496.4 %collective-permute-start.23 = (bf16[128,128]{1,0:T(8,128)(2,1)S(1)}, bf16[128,128]{1,0:T(8,128)(2,1)S(1)}, u32[]{:S(2)}, u32[]{:S(2)}) collective-permute-start(bf16[128,128]{1,0:T(8,128)(2,1)S(1)} %get-tuple-element.580), channel_id=1, source_target_pairs={{12,0},{16,4},{20,8},{24,12},{28,16},{32,20},{36,24},{40,28},{44,3... | collective-permute-start | bytes 98312 | tf_op jit(solution)/shard_map/ppermute | solution.py:18
  368.0 502.7 %collective-permute-start.24 = (bf16[128,128]{1,0:T(8,128)(2,1)S(1)}, bf16[128,128]{1,0:T(8,128)(2,1)S(1)}, u32[]{:S(2)}, u32[]{:S(2)}) collective-permute-start(bf16[128,128]{1,0:T(8,128)(2,1)S(1)} %get-tuple-element.579), channel_id=1, source_target_pairs={{16,0},{20,4},{24,8},{28,12},{32,16},{36,20},{40,24},{44,28},{48,3... | collective-permute-start | bytes 98312 | tf_op jit(solution)/shard_map/ppermute | solution.py:18
  369.3 502.7 %collective-permute-start.25 = (bf16[128,128]{1,0:T(8,128)(2,1)S(1)}, bf16[128,128]{1,0:T(8,128)(2,1)S(1)}, u32[]{:S(2)}, u32[]{:S(2)}) collective-permute-start(bf16[128,128]{1,0:T(8,128)(2,1)S(1)} %get-tuple-element.578), channel_id=1, source_target_pairs={{20,0},{24,4},{28,8},{32,12},{36,16},{40,20},{44,24},{48,28},{52,3... | collective-permute-start | bytes 98312 | tf_op jit(solution)/shard_map/ppermute | solution.py:18
  370.6 0.9 copy-start.1
  372.8 503.5 %copy-start = (bf16[128,1,128]{2,0,1:T(8,128)(2,1)S(1)}, bf16[128,1,128]{2,0,1:T(8,128)(2,1)}, u32[]{:S(2)}) copy-start(bf16[128,1,128]{2,0,1:T(8,128)(2,1)} %param.20) | copy-start | bytes 98308
  858.5 14.8 %collective-permute-start.26 = (bf16[128,128]{1,0:T(8,128)(2,1)S(1)}, bf16[128,128]{1,0:T(8,128)(2,1)S(1)}, u32[]{:S(2)}, u32[]{:S(2)}) collective-permute-start(bf16[128,128]{1,0:T(8,128)(2,1)S(1)} %get-tuple-element.577), channel_id=1, source_target_pairs={{24,0},{28,4},{32,8},{36,12},{40,16},{44,20},{48,24},{52,28},{56,3... | collective-permute-start | bytes 98312 | tf_op jit(solution)/shard_map/ppermute | solution.py:18
  859.8 14.8 %collective-permute-start.27 = (bf16[128,128]{1,0:T(8,128)(2,1)S(1)}, bf16[128,128]{1,0:T(8,128)(2,1)S(1)}, u32[]{:S(2)}, u32[]{:S(2)}) collective-permute-start(bf16[128,128]{1,0:T(8,128)(2,1)S(1)} %get-tuple-element.576), channel_id=1, source_target_pairs={{28,0},{32,4},{36,8},{40,12},{44,16},{48,20},{52,24},{56,28},{60,3... | collective-permute-start | bytes 98312 | tf_op jit(solution)/shard_map/ppermute | solution.py:18
  861.7 33.3 %copy-start.8 = (bf16[2,1,128]{2,0,1:T(2,128)(2,1)S(1)}, bf16[2,1,128]{2,0,1:T(2,128)(2,1)}, u32[]{:S(2)}) copy-start(bf16[2,1,128]{2,0,1:T(2,128)(2,1)} %param.25) | copy-start | bytes 1540
  863.1 13.4 %collective-permute-start.28 = (bf16[128,128]{1,0:T(8,128)(2,1)S(1)}, bf16[128,128]{1,0:T(8,128)(2,1)S(1)}, u32[]{:S(2)}, u32[]{:S(2)}) collective-permute-start(bf16[128,128]{1,0:T(8,128)(2,1)S(1)} %get-tuple-element.568), channel_id=1, source_target_pairs={{4,0},{8,4},{12,8},{16,12},{20,16},{24,20},{28,24},{32,28},{36,32}... | collective-permute-start | bytes 98312 | tf_op jit(solution)/shard_map/ppermute | solution.py:18
  870.7 7.1 collective-permute-start.29
  872.0 7.1 collective-permute-start.30
  873.3 7.5 collective-permute-start.31
  874.6 10.3 %collective-permute-start.32 = (bf16[128,128]{1,0:T(8,128)(2,1)S(1)}, bf16[128,128]{1,0:T(8,128)(2,1)S(1)}, u32[]{:S(2)}, u32[]{:S(2)}) collective-permute-start(bf16[128,128]{1,0:T(8,128)(2,1)S(1)} %get-tuple-element.571), channel_id=1, source_target_pairs={{20,0},{24,4},{28,8},{32,12},{36,16},{40,20},{44,24},{48,28},{52,3... | collective-permute-start | bytes 98312 | tf_op jit(solution)/shard_map/ppermute | solution.py:18
  876.5 11.1 %collective-permute-start.33 = (bf16[128,128]{1,0:T(8,128)(2,1)S(1)}, bf16[128,128]{1,0:T(8,128)(2,1)S(1)}, u32[]{:S(2)}, u32[]{:S(2)}) collective-permute-start(bf16[128,128]{1,0:T(8,128)(2,1)S(1)} %get-tuple-element.570), channel_id=1, source_target_pairs={{24,0},{28,4},{32,8},{36,12},{40,16},{44,20},{48,24},{52,28},{56,3... | collective-permute-start | bytes 98312 | tf_op jit(solution)/shard_map/ppermute | solution.py:18
  877.8 15.0 %collective-permute-start.34 = (bf16[128,128]{1,0:T(8,128)(2,1)S(1)}, bf16[128,128]{1,0:T(8,128)(2,1)S(1)}, u32[]{:S(2)}, u32[]{:S(2)}) collective-permute-start(bf16[128,128]{1,0:T(8,128)(2,1)S(1)} %get-tuple-element.569), channel_id=1, source_target_pairs={{28,0},{32,4},{36,8},{40,12},{44,16},{48,20},{52,24},{56,28},{60,3... | collective-permute-start | bytes 98312 | tf_op jit(solution)/shard_map/ppermute | solution.py:18
Sparse Core Ops, SparseCore 0:
  363.5 318.1 all-reduce.7
where the time goes:
time: 1020 us; the launch traced here: 1010 us
  blocking collectives  751 us (74%)
  starting transfers between devices  135 us (13%)
  other arithmetic  43.4 us (4%)
  local copies, waits for them, and re-layouts  22.6 us (2%)
  matrix products  22.5 us (2%)
  waiting for transfers between devices  16.9 us (2%)
  between operations  16.4 us (2%)
    unnamed x1, blocking collectives  486 us
    ppermute x35, starting transfers between devices, shifted(): lax.ppermute(value, axis, [(source, source + steps) for source in range(l...  135 us
    psum x1, blocking collectives, per_device(): sum_q, sum_k = lax.psum((gain_part_q, gain_bk + gain_pk), ('ctx', 'head'))  111 us
    all_gather x1, blocking collectives, per_device(): lax.all_gather(prompt_v[:, 0], 'ctx', axis=0, tiled=True)  81.3 us
    all_gather x1, blocking collectives, per_device(): lax.all_gather(rotated_pk, 'ctx', axis=0, tiled=True)  72.9 us
  transfers between devices with their start and end apart: 36, of which 11 were waited for; matrix products, arithmetic and copies ran while one was open for 4% of the time, Pallas kernels for 0%

commit v1 on v0

v1 whole, which is shorter than its diff:
```python
import math

import numpy as np

import jax
import jax.numpy as jnp
from jax import lax
from jax.experimental import pallas as pl
from jax.experimental.pallas import tpu as pltpu
from jax.sharding import PartitionSpec as P

HD = 128
G = 8
BLK = 128
SUB = 8
PFX = 256
EPS = 1e-06
THETA = 1000000.0
Y = 4
Z = 16
GRP = 2 * Y
X = 4
NCTX = Y * Z * 2
ROWS = BLK * G
PROWS = 128
ALLR = ROWS + PROWS
KEYS = PFX + SUB * BLK
SCALE = HD ** (-0.5)
EXP2_SCALE = SCALE * math.log2(math.e)
MESH = pl.DeviceIdType.MESH
F32 = jnp.float32
BF16 = jnp.bfloat16


def prompt_order():
    p = np.arange(PFX)
    return (p // 4 % 4) * 64 + (p // 16) * 4 + p % 4


def tables():
    freq = THETA ** (-(np.arange(HD // 2, dtype=np.float64) * 2.0) / HD)

    def pair(positions):
        angle = positions[:, None].astype(np.float64) * freq[None, :]
        cosine, sine = np.cos(angle), np.sin(angle)
        return np.stack(
            [np.concatenate([cosine, cosine], 1), np.concatenate([-sine, sine], 1)]
        ).astype(np.float32)

    offset = pair(np.arange(BLK))
    level = pair(np.arange(16) * BLK)
    prompt = pair(prompt_order())
    return offset, level, prompt


def norm(x):
    inverse = lax.rsqrt(jnp.mean(x * x, axis=-1, keepdims=True) + EPS)
    return x * inverse, inverse


def swap(x):
    return pltpu.roll(x, HD // 2, 1)


def rotate(x, c, s):
    return x * c + swap(x) * s


def unrotate(x, c, s):
    return x * c - swap(x) * s


def norm_back(grad, unit, inverse, gain, c, s):
    g = unrotate(grad, c, s)
    u = g * gain
    raw = (u - unit * jnp.mean(u * unit, axis=-1, keepdims=True)) * inverse
    return raw, jnp.sum(g * unit, axis=0, keepdims=True)


def nt(a, b):
    return lax.dot_general(a, b, (((1,), (1,)), ((), ())), preferred_element_type=F32)


def nn(a, b):
    return lax.dot_general(a, b, (((1,), (0,)), ((), ())), preferred_element_type=F32)


def kernel(
    q_ref, k_hbm, v_hbm, o_ref, do_ref, pq_ref, pk_ref, pv_ref, po_ref, pdo_ref,
    gains_ref, par_ref, depth_ref, toff_ref, tlev_ref, tpr_ref,
    dq_ref, dk_ref, dv_ref, pdq_ref, pdk_ref, pdv_ref, gg_ref,
    kv, parw, grp, pkv,
    qrot, qunit, qinv, dor, delta, krot, krott, kunit, kinv, ctab, stab, thr, e_s, tot, dqt,
    scr, pscr, vp,
    wterm, ownk, ownv, prx, mtx, mrx, pterm, rs1, rs2t, rs2, g1, g2,
    s_loc, s_kv, r_kv, s_par, r_par, s_ag1, r_ag1, s_ag2, r_ag2,
    s_p, r_p, s_m, r_m, s_rs1, r_rs1, s_rs2, r_rs2, s_g1, r_g1, s_g2, r_g2,
):
    me = lax.axis_index("ctx")
    hx = lax.axis_index("head")
    y = me // (2 * Z)
    z = lax.rem(me // 2, Z)
    c = lax.rem(me, 2)
    gi = y * 2 + c
    partner = me + 1 - 2 * c
    base = gi * 2

    def at(offset):
        return lax.rem(me + (offset + NCTX), NCTX)

    def grp_dev(index):
        return ((index // 2) * Z + z) * 2 + lax.rem(index, 2)

    def z_dev(index):
        return (y * Z + index) * 2 + c

    def copy(src, dst, ssem, rsem, device, head=None):
        where = {"ctx": device} if head is None else {"ctx": device, "head": head}
        return pltpu.make_async_remote_copy(
            src_ref=src, dst_ref=dst, send_sem=ssem, recv_sem=rsem,
            device_id=where, device_id_type=MESH,
        )

    own = [
        pltpu.make_async_copy(k_hbm, kv.at[0, 0], s_loc.at[0]),
        pltpu.make_async_copy(v_hbm, kv.at[0, 1], s_loc.at[1]),
    ]
    for cp in own:
        cp.start()
    barrier = pltpu.get_barrier_semaphore()

    def greet(device, head=None):
        where = {"ctx": device} if head is None else {"ctx": device, "head": head}
        pl.semaphore_signal(barrier, inc=1, device_id=where, device_id_type=MESH)

    for offset in (-7, -6, -5, -4, -3, -2, -1, 1, 2):
        greet(at(offset))

    @pl.loop(1, Z)
    def _(j):
        greet(z_dev(lax.rem(z + j, Z)))

    @pl.loop(1, GRP * X)
    def _(j):
        other = lax.rem(hx * GRP + gi + j, GRP * X)
        greet(grp_dev(lax.rem(other, GRP)), other // GRP)

    parw[0] = jnp.full((1, HD), par_ref[0], jnp.int32)
    row16 = lax.broadcasted_iota(jnp.int32, (16, HD), 0)

    def spread(two_rows):
        x = two_rows.astype(F32)
        first = jnp.broadcast_to(x[0:1], (16, HD))
        second = jnp.broadcast_to(x[1:2], (16, HD))
        return jnp.where(row16 == base, first, jnp.where(row16 == base + 1, second, 0.0))

    grp[gi, 0:16, :] = spread(pk_ref[...]).astype(BF16)
    grp[gi, 16:32, :] = spread(pv_ref[...]).astype(BF16)

    gain_q = gains_ref[0:1, :]
    gain_k = gains_ref[1:2, :]
    lane1 = lax.broadcasted_iota(jnp.int32, (1, HD), 1)
    level = (depth_ref[...] - lane1) >> 7

    def level_rows(lv):
        cl = jnp.zeros((1, HD), F32)
        sl = jnp.zeros((1, HD), F32)
        for n in range(1, SUB + 2):
            cl = jnp.where(lv == n, tlev_ref[0, n : n + 1, :], cl)
            sl = jnp.where(lv == n, tlev_ref[1, n : n + 1, :], sl)
        return cl, sl

    def block_tables(lv):
        cl, sl = level_rows(lv)
        co, so = toff_ref[0], toff_ref[1]
        return co * cl - so * sl, so * cl + co * sl

    c0, s0 = block_tables(level)
    ctab[0] = c0
    stab[0] = s0

    @pl.loop(0, G)
    def _(g):
        lanes = pl.ds(pl.multiple_of(g * HD, HD), HD)
        rows = pl.ds(pl.multiple_of(g * BLK, BLK), BLK)
        unit, inverse = norm(q_ref[:, lanes].astype(F32))
        qunit[rows, :] = unit
        qinv[rows, :] = jnp.broadcast_to(inverse, (BLK, HD))
        qrot[rows, :] = rotate(unit * gain_q, ctab[0], stab[0]).astype(BF16)
        d = do_ref[:, lanes]
        dor[rows, :] = d
        prod = d.astype(F32) * o_ref[:, lanes].astype(F32)
        delta[:, lanes] = jnp.sum(prod.T, axis=0, keepdims=True)

    def to_rows(ref):
        x = ref[...].astype(F32)
        for g in range(G):
            scr[2 * g : 2 * g + 2, :] = x[:, g * HD : (g + 1) * HD]
        return scr[0:16, :]

    pslot = z * 16 + base
    odd = lax.rem(row16, 2) == 1

    def prow(n):
        first = jnp.broadcast_to(tpr_ref[n, pl.ds(pslot, 1), :], (16, HD))
        second = jnp.broadcast_to(tpr_ref[n, pl.ds(pslot + 1, 1), :], (16, HD))
        return jnp.where(odd, second, first)

    pc16, ps16 = prow(0), prow(1)
    prest = pl.ds(ROWS + 16, PROWS - 16)
    punit, pinverse = norm(to_rows(pq_ref))
    qrot[ROWS : ROWS + 16, :] = rotate(punit * gain_q, pc16, ps16).astype(BF16)
    qrot[prest, :] = jnp.zeros((PROWS - 16, HD), BF16)
    pd = to_rows(pdo_ref)
    dor[ROWS : ROWS + 16, :] = pd.astype(BF16)
    dor[prest, :] = jnp.zeros((PROWS - 16, HD), BF16)
    pscr[...] = jnp.zeros((PROWS, HD), F32)
    pscr[0:16, :] = pd * to_rows(po_ref)
    delta[:, ROWS:] = jnp.sum(pscr[...].T, axis=0, keepdims=True)
    for cp in own:
        cp.wait()
    pl.semaphore_wait(barrier, 9 + (Z - 1) + (GRP * X - 1))

    def kv_copy(op, n, src, dst, device):
        return copy(kv.at[src, n], kv.at[dst, n], s_kv.at[op, n], r_kv.at[dst, n], device)

    def kv_arrived(slot, n):
        copy(kv.at[slot, n], kv.at[slot, n], s_kv.at[0, n], r_kv.at[slot, n], partner).wait_recv()

    sent = []

    def send(cp):
        cp.start()
        sent.append(cp)

    for n in range(2):
        send(kv_copy(0, n, 0, 2, at(2)))

    @pl.when(c == 0)
    def _():
        for n in range(2):
            kv_copy(1, n, 0, 1, partner).start()

    for j in range(1, GRP):
        send(copy(grp.at[gi], grp.at[gi], s_ag1.at[j], r_ag1.at[gi], grp_dev(lax.rem(gi + j, GRP))))
    for d in range(1, SUB):
        send(copy(parw.at[0], parw.at[d], s_par.at[d], r_par.at[d], at(d)))

    for n in range(2):
        kv_arrived(2, n)
        send(kv_copy(2, n, 2, 4, at(2)))
        send(kv_copy(3, n, 2, 3 - 2 * c, partner))
    for j in range(1, GRP):
        slot = lax.rem(gi + j, GRP)
        copy(grp.at[slot], grp.at[slot], s_ag1.at[j], r_ag1.at[slot], partner).wait_recv()
    tile = grp[0].astype(F32)
    for j in range(1, GRP):
        tile = tile + grp[j].astype(F32)
    pkv[z] = tile.astype(BF16)

    @pl.loop(1, Z)
    def _(j):
        copy(pkv.at[z], pkv.at[z], s_ag2.at[j], r_ag2.at[z], z_dev(lax.rem(z + j, Z))).start()

    for n in range(2):
        kv_arrived(4, n)
        send(kv_copy(4, n, 4, 6, at(2)))
        send(kv_copy(5, n, 4, 5 - 2 * c, partner))
    for n in range(2):
        kv_arrived(6, n)
        send(kv_copy(6, n, 6, 7, at(1)))

    @pl.when(c == 1)
    def _():
        for n in range(2):
            kv_copy(7, n, 6, 5, partner).start()

    for d in (1, 3, 5, 7):
        for n in range(2):
            kv_arrived(d, n)
    for d in range(1, SUB):
        copy(parw.at[d], parw.at[d], s_par.at[d], r_par.at[d], partner).wait_recv()

    @pl.loop(1, Z)
    def _(j):
        slot = lax.rem(z + j, Z)
        copy(pkv.at[slot], pkv.at[slot], s_ag2.at[j], r_ag2.at[slot], z_dev(slot)).wait_recv()

    block = me + PFX // BLK
    current = jnp.full((1, HD), block, jnp.int32)
    seen = [jnp.zeros((1, HD), jnp.int32) for _ in range(SUB)]
    levels = [jnp.zeros((1, HD), jnp.int32) for _ in range(SUB)]
    above = [parw[d] for d in range(SUB)]
    for step in range(SUB + 1):
        branchy = current >= PFX // BLK
        upward = jnp.zeros((1, HD), jnp.int32)
        for d in range(SUB):
            match = (current == block - d) & branchy
            seen[d] = jnp.where(match, 1, seen[d])
            levels[d] = jnp.where(match, level - step, levels[d])
            upward = jnp.where(match, above[d], upward)
        current = jnp.where(branchy, upward, current)
    fork = current

    def wide(x):
        return jnp.concatenate([x] * G, axis=1)

    thr[0] = jnp.where(wide(seen[0]) == 1, wide(lane1), -1)
    for d in range(1, SUB):
        thr[d] = jnp.where(wide(seen[d]) == 1, BLK, -1)
    thr_prompt = jnp.concatenate(
        [wide(BLK * (fork + 1) - 1), me * 2 + lax.rem(lane1, 2)], axis=1
    )

    pcos, psin = tpr_ref[0], tpr_ref[1]
    pk_all = jnp.concatenate([pkv[n, 0:16, :] for n in range(Z)], axis=0).astype(F32)
    for n in range(Z):
        vp[n * 16 : (n + 1) * 16, :] = pkv[n, 16:32, :]
    pkunit, _ = norm(pk_all)
    rot = rotate(pkunit * gain_k, pcos, psin)
    krot[0:PFX, :] = rot.astype(BF16)
    krott[:, 0:PFX] = rot.T.astype(BF16)
    kunit[0:PFX, :] = pkunit
    for d in range(SUB):
        rows = slice(PFX + d * BLK, PFX + (d + 1) * BLK)
        if d:
            cd, sd = block_tables(levels[d])
            ctab[d] = cd
            stab[d] = sd
        unit, inverse = norm(kv[d, 0].astype(F32))
        if d == 0:
            kinv[...] = jnp.broadcast_to(inverse, (BLK, HD))
        kunit[rows, :] = unit
        rot = rotate(unit * gain_k, ctab[d], stab[d])
        krot[rows, :] = rot.astype(BF16)
        krott[:, rows] = rot.T.astype(BF16)

    t_key = lax.broadcasted_iota(jnp.int32, (PFX, ALLR), 0)
    t_key = ((t_key >> 2) & 3) * 64 + (t_key >> 4) * 4 + (t_key & 3)
    s = nt(krot[0:PFX, :], qrot[...])
    e = jnp.where(t_key <= thr_prompt, jnp.exp2(s * EXP2_SCALE), 0.0)
    e_s[0:PFX, :] = e
    tot[...] = jnp.sum(e, axis=0, keepdims=True)
    offs = lax.broadcasted_iota(jnp.int32, (BLK, ROWS), 0)

    @pl.loop(0, SUB)
    def _(d):
        rows = pl.ds(pl.multiple_of(PFX + d * BLK, BLK), BLK)
        s = nt(krot[rows, :], qrot[0:ROWS, :])
        e = jnp.where(offs <= thr[d], jnp.exp2(s * EXP2_SCALE), 0.0)
        e_s[rows, 0:ROWS] = e
        tot[:, 0:ROWS] += jnp.sum(e, axis=0, keepdims=True)

    tot[...] = 1.0 / tot[...]

    def back(krows, vals, width):
        p = e_s[krows, 0:width] * tot[:, 0:width]
        d = dor[0:width, :]
        dv = nn(p.astype(BF16), d)
        dp = nt(vals, d)
        ds = (p * (dp - delta[:, 0:width])).astype(BF16)
        dk = nn(ds, qrot[0:width, :]) * SCALE
        return dk, dv, nn(krott[:, krows], ds)

    dk, dv, dqt0 = back(slice(0, PFX), vp[...], ALLR)
    dqt[...] = dqt0
    for n in range(Z):
        pterm[n, 0:16, :] = dk[n * 16 : (n + 1) * 16].astype(BF16)
        pterm[n, 16:32, :] = dv[n * 16 : (n + 1) * 16].astype(BF16)
    gk = jnp.sum(unrotate(dk, pcos, psin) * kunit[0:PFX, :], axis=0, keepdims=True)

    @pl.loop(1, Z)
    def _(j):
        other = lax.rem(z + j, Z)
        copy(pterm.at[other], rs1.at[z], s_rs1.at[j], r_rs1.at[z], z_dev(other)).start()

    for d in range(SUB - 1, -1, -1):
        rows = slice(PFX + d * BLK, PFX + (d + 1) * BLK)
        dk, dv, part = back(rows, kv[d, 1], ROWS)
        dqt[:, 0:ROWS] += part
        if d:
            wterm[d, 0] = dk.astype(BF16)
            wterm[d, 1] = dv.astype(BF16)
        else:
            ownk[...] = dk
            ownv[...] = dv
        gk = gk + jnp.sum(unrotate(dk, ctab[d], stab[d]) * kunit[rows, :], axis=0, keepdims=True)

    for n in range(2):
        send(copy(wterm.at[7, n], prx.at[3, n], s_p.at[3, n], r_p.at[3, n], at(-1)))
    for slot in (2, 1, 0):
        for n in range(2):
            send(copy(wterm.at[2 * slot + 1, n], prx.at[slot, n], s_p.at[slot, n], r_p.at[slot, n], partner))

    gq = jnp.zeros((1, HD), F32)
    for g in range(G):
        rows = slice(g * BLK, (g + 1) * BLK)
        grad = dqt[:, rows].T * SCALE
        raw, part = norm_back(grad, qunit[rows, :], qinv[rows, :], gain_q, ctab[0], stab[0])
        dq_ref[:, rows] = raw.astype(BF16)
        gq = gq + part
    grad = dqt[:, ROWS:].T[0:16] * SCALE
    raw, part = norm_back(grad, punit, pinverse, gain_q, pc16, ps16)
    gq = gq + part
    scr[...] = raw
    for g in range(G):
        pdq_ref[:, g * HD : (g + 1) * HD] = scr[2 * g : 2 * g + 2, :].astype(BF16)

    row8 = lax.broadcasted_iota(jnp.int32, (8, HD), 0)
    g1[z] = jnp.where(row8 == 0, gq, jnp.where(row8 == 1, gk, 0.0))

    @pl.loop(1, Z)
    def _(j):
        copy(g1.at[z], g1.at[z], s_g1.at[j], r_g1.at[z], z_dev(lax.rem(z + j, Z))).start()

    def p_arrived(slot, n):
        copy(prx.at[slot, n], prx.at[slot, n], s_p.at[slot, n], r_p.at[slot, n], partner).wait_recv()

    def m_arrived(k, n):
        copy(mrx.at[k, n], mrx.at[k, n], s_m.at[k, n], r_m.at[k, n], partner).wait_recv()

    for slot in range(4):
        for n in range(2):
            p_arrived(slot, n)
    for k in (3, 2, 1):
        for n in range(2):
            if k < 3:
                m_arrived(k, n)
            value = wterm[2 * k, n].astype(F32) + prx[k - c, n].astype(F32)
            if k == 3:
                value = value + jnp.where(c == 1, prx[3, n].astype(F32), 0.0)
            else:
                value = value + mrx[k, n].astype(F32)
            mtx[k - 1, n] = value.astype(BF16)
        for n in range(2):
            send(copy(mtx.at[k - 1, n], mrx.at[k - 1, n], s_m.at[k - 1, n], r_m.at[k - 1, n], at(-2)))
        if k == 3:

            @pl.loop(1, Z)
            def _(j):
                slot = lax.rem(z + j, Z)
                copy(rs1.at[slot], rs1.at[slot], s_rs1.at[j], r_rs1.at[slot], z_dev(slot)).wait_recv()

            rs1[z] = pterm[z]
            total = rs1[0].astype(F32)
            for n in range(1, Z):
                total = total + rs1[n].astype(F32)
            rs2[gi] = total.astype(BF16)
            for j in range(1, GRP):
                send(copy(rs2.at[gi], rs2.at[gi], s_rs2.at[j], r_rs2.at[gi], grp_dev(lax.rem(gi + j, GRP))))
        if k == 2:

            @pl.loop(1, Z)
            def _(j):
                slot = lax.rem(z + j, Z)
                copy(g1.at[slot], g1.at[slot], s_g1.at[j], r_g1.at[slot], z_dev(slot)).wait_recv()

            total = g1[0]
            for n in range(1, Z):
                total = total + g1[n]
            xg = hx * GRP + gi
            g2[xg] = total

            @pl.loop(1, GRP * X)
            def _(j):
                other = lax.rem(xg + j, GRP * X)
                copy(
                    g2.at[xg], g2.at[xg], s_g2.at[j], r_g2.at[xg], grp_dev(lax.rem(other, GRP)), other // GRP
                ).start()

    for n, total_ref in ((0, ownk), (1, ownv)):
        m_arrived(0, n)
        total_ref[...] += mrx[0, n].astype(F32)

        @pl.when(c == 0)
        def _():
            total_ref[...] += prx[0, n].astype(F32)

    raw, _ = norm_back(
        ownk[...], kunit[PFX : PFX + BLK, :], kinv[...], gain_k, ctab[0], stab[0]
    )
    dk_ref[...] = raw.astype(BF16)
    dv_ref[...] = ownv[...].astype(BF16)

    for j in range(1, GRP):
        slot = lax.rem(gi + j, GRP)
        copy(rs2.at[slot], rs2.at[slot], s_rs2.at[j], r_rs2.at[slot], partner).wait_recv()
    total = rs2[0].astype(F32)
    for j in range(1, GRP):
        total = total + rs2[j].astype(F32)

    def pick(x):
        first = jnp.sum(jnp.where(row16 == base, x, 0.0), axis=0, keepdims=True)
        second = jnp.sum(jnp.where(row16 == base + 1, x, 0.0), axis=0, keepdims=True)
        return jnp.concatenate([first, second], axis=0)

    ptk = pick(total[0:16])
    ptv = pick(total[16:32])
    unit2, inverse2 = norm(pk_ref[...].astype(F32))
    raw, _ = norm_back(ptk, unit2, inverse2, gain_k, pc16[0:2], ps16[0:2])
    pdk_ref[...] = raw.astype(BF16)
    pdv_ref[...] = ptv.astype(BF16)

    @pl.loop(1, GRP * X)
    def _(j):
        slot = lax.rem(hx * GRP + gi + j, GRP * X)
        copy(g2.at[slot], g2.at[slot], s_g2.at[j], r_g2.at[slot], partner).wait_recv()

    total = g2[0]
    for n in range(1, GRP * X):
        total = total + g2[n]
    count = (NCTX * (BLK + 2)) * X
    factor = jnp.where(row8 == 0, (count * G) ** (-0.5), count ** (-0.5))
    gg_ref[...] = (total * factor)[0:2]

    for cp in sent:
        cp.wait_send()

    @pl.when(c == 0)
    def _():
        for n in range(2):
            kv_copy(1, n, 0, 1, partner).wait_send()

    @pl.when(c == 1)
    def _():
        for n in range(2):
            kv_copy(7, n, 6, 5, partner).wait_send()

    @pl.loop(1, Z)
    def _(j):
        copy(pkv.at[z], pkv.at[z], s_ag2.at[j], r_ag2.at[z], partner).wait_send()
        copy(pterm.at[z], rs1.at[z], s_rs1.at[j], r_rs1.at[z], partner).wait_send()
        copy(g1.at[z], g1.at[z], s_g1.at[j], r_g1.at[z], partner).wait_send()

    @pl.loop(1, GRP * X)
    def _(j):
        copy(g2.at[0], g2.at[0], s_g2.at[j], r_g2.at[0], partner).wait_send()


def per_device(
    branch_q, branch_k, branch_v, branch_o, branch_dout,
    prompt_q, prompt_k, prompt_v, prompt_o, prompt_dout, gains, parents, depth,
):
    offset, level, prompt = tables()
    vmem = pl.BlockSpec(memory_space=pltpu.VMEM)
    hbm = pl.BlockSpec(memory_space=pl.ANY)
    smem = pl.BlockSpec(memory_space=pltpu.SMEM)
    dma = pltpu.SemaphoreType.DMA
    vm = pltpu.VMEM
    outs = pl.pallas_call(
        kernel,
        out_shape=(
            jax.ShapeDtypeStruct((BLK, G * HD), BF16),
            jax.ShapeDtypeStruct((BLK, HD), BF16),
            jax.ShapeDtypeStruct((BLK, HD), BF16),
            jax.ShapeDtypeStruct((2, G * HD), BF16),
            jax.ShapeDtypeStruct((2, HD), BF16),
            jax.ShapeDtypeStruct((2, HD), BF16),
            jax.ShapeDtypeStruct((2, HD), F32),
        ),
        in_specs=[vmem, hbm, hbm] + [vmem] * 8 + [smem] + [vmem] * 4,
        out_specs=(vmem,) * 7,
        scratch_shapes=[
            vm((SUB, 2, BLK, HD), BF16),
            vm((SUB, 1, HD), jnp.int32),
            vm((GRP, 32, HD), BF16),
            vm((Z, 32, HD), BF16),
            vm((ALLR, HD), BF16),
            vm((ROWS, HD), F32),
            vm((ROWS, HD), F32),
            vm((ALLR, HD), BF16),
            vm((1, ALLR), F32),
            vm((KEYS, HD), BF16),
            vm((HD, KEYS), BF16),
            vm((KEYS, HD), F32),
            vm((BLK, HD), F32),
            vm((SUB, BLK, HD), F32),
            vm((SUB, BLK, HD), F32),
            vm((SUB, 1, ROWS), jnp.int32),
            vm((KEYS, ALLR), F32),
            vm((1, ALLR), F32),
            vm((HD, ALLR), F32),
            vm((16, HD), F32),
            vm((PROWS, HD), F32),
            vm((PFX, HD), BF16),
            vm((SUB, 2, BLK, HD), BF16),
            vm((BLK, HD), F32),
            vm((BLK, HD), F32),
            vm((4, 2, BLK, HD), BF16),
            vm((3, 2, BLK, HD), BF16),
            vm((3, 2, BLK, HD), BF16),
            vm((Z, 32, HD), BF16),
            vm((Z, 32, HD), BF16),
            vm((8, HD), F32),
            vm((GRP, 32, HD), BF16),
            vm((Z, 8, HD), F32),
            vm((GRP * X, 8, HD), F32),
            dma((2,)),
            dma((8, 2)), dma((SUB, 2)),
            dma((SUB,)), dma((SUB,)),
            dma((GRP,)), dma((GRP,)),
            dma((Z,)), dma((Z,)),
            dma((4, 2)), dma((4, 2)),
            dma((3, 2)), dma((3, 2)),
            dma((Z,)), dma((Z,)),
            dma((GRP,)), dma((GRP,)),
            dma((Z,)), dma((Z,)),
            dma((GRP * X,)), dma((GRP * X,)),
        ],
        compiler_params=pltpu.CompilerParams(
            collective_id=0, has_side_effects=True, vmem_limit_bytes=60 * 1024 * 1024
        ),
        name="tree_back",
    )(
        branch_q[:, 0], branch_k[:, 0], branch_v[:, 0], branch_o[:, 0], branch_dout[:, 0],
        prompt_q[:, 0], prompt_k[:, 0], prompt_v[:, 0], prompt_o[:, 0], prompt_dout[:, 0],
        gains, parents, depth.reshape(1, BLK),
        jnp.asarray(offset), jnp.asarray(level), jnp.asarray(prompt),
    )
    dq, dk, dv, pdq, pdk, pdv, gain_grads = outs
    return (
        dq[:, None], dk[:, None], dv[:, None], pdq[:, None], pdk[:, None], pdv[:, None], gain_grads,
    )


def solution(mesh):
    tok = P("ctx", "head", None)
    return jax.shard_map(
        per_device,
        mesh=mesh,
        in_specs=(tok,) * 10 + (P(), P("ctx"), P("ctx")),
        out_specs=(tok,) * 6 + (P(),),
        check_vma=False,
    )
```

time: 1020 us -> 69.3 us (0.07)
  blocking collectives: 751 us -> 0 us
  starting transfers between devices: 135 us -> 0 us
  Pallas kernels: 0 us -> 62.1 us
  other arithmetic: 43.4 us -> 0 us
  matrix products: 22.5 us -> 0 us
  local copies, waits for them, and re-layouts: 22.6 us -> 5.67 us
  waiting for transfers between devices: 16.9 us -> 0 us
  between operations: 16.4 us -> 1.31 us
    unnamed x1 -> x0, blocking collectives: 486 us -> none
    all_gather x2 -> x0, blocking collectives: 154 us -> none  [the longest x1 81.3 us: per_device(): lax.all_gather(prompt_v[:, 0], 'ctx', axis=0, tiled=True)]
    ppermute x35 -> x0, starting transfers between devices: 135 us -> none  [shifted(): lax.ppermute(value, axis, [(source, source + steps) for source in range(l...]
    psum x1 -> x0, blocking collectives: 111 us -> none  [per_device(): sum_q, sum_k = lax.psum((gain_part_q, gain_bk + gain_pk), ('ctx', 'head'))]
    pallas_call x0 -> x1, Pallas kernels: none -> 62.1 us  [per_device(): pl.pallas_call(kernel, out_shape=(jax.ShapeDtypeStruct((BLK, G * HD), BF1...]
    dot_general x30 -> x0, matrix products: 22.5 us -> none  [the longest x5 5.81 us: back_piece(): jnp.einsum('qd,kd->qk', grad_rows, value_piece, preferred_element_type=jn...]
    ppermute x35 -> x0, waiting for transfers between devices: 16.8 us -> none  [shifted(): lax.ppermute(value, axis, [(source, source + steps) for source in range(l...]
  transfers between devices with their start and end apart: 36 -> 0, of which waited for: 11 -> 0; matrix products, arithmetic and copies ran while one was open for 4% -> 0% of each run, Pallas kernels for 0% -> 0%
where the time goes in v1:
time: 69.3 us; the launch traced here: 69 us
  Pallas kernels  62.1 us (90%)
  local copies, waits for them, and re-layouts  5.67 us (8%)
  between operations  1.31 us (2%)
    pallas_call x1, Pallas kernels, per_device(): pl.pallas_call(kernel, out_shape=(jax.ShapeDtypeStruct((BLK, G * HD), BF1...  62.1 us
    unnamed x19, local copies, waits for them, and re-layouts  5.67 us

profile of v1, /device:TPU:1, one launch (start us, length us, event | category | flops | bytes accessed | tf_op | source)
XLA Modules:
  0.0 69.0 jit_solution(8420864495024767069)
XLA Ops:
  1.3 62.1 %tree_back.1 = (bf16[128,1024]{1,0:T(8,128)(2,1)}, bf16[128,128]{1,0:T(8,128)(2,1)}, bf16[128,128]{1,0:T(8,128)(2,1)}, bf16[2,1024]{1,0:T(2,128)(2,1)}, bf16[2,1...) custom-call(bf16[128,1024]{1,0:T(8,128)(2,1)} %bitcast.18, bf16[128,128]{1,0:T(8,128)(2,1)} %bitcast.21, ...), custom_call_target="tpu_custom_call" | custom-call | tf_op jit(solution)/shard_map/tree_back/pallas_call | solution.py:550
  63.4 0.0 copy-start.1
  63.4 1.7 %copy.31 = bf16[128,1,1024]{2,0,1:T(8,128)(2,1)} copy(bf16[128,1,1024]{2,0,1:T(8,128)(2,1)} %bitcast.17) | data formatting | bytes 524288
  65.0 0.0 copy-done.1
  65.0 0.0 copy-start
  65.0 0.6 copy.32
  65.7 0.2 copy-done
  65.8 0.0 copy-start.2
  65.8 0.6 copy.33
  66.4 0.1 copy-done.2
  66.5 0.0 copy-start.5
  66.5 0.6 copy.34
  67.1 0.1 copy-done.5
  67.2 0.0 copy-start.4
  67.2 0.5 copy.35
  67.7 0.1 copy-done.4
  67.8 0.0 copy-start.3
  67.8 0.5 copy.36
  68.3 0.2 copy-done.3
  68.5 0.6 copy.37
Async XLA Ops:
  63.4 1.7 %copy-start.1 = (bf16[128,128]{1,0:T(8,128)(2,1)S(1)}, bf16[128,128]{1,0:T(8,128)(2,1)}, u32[]{:S(2)}) copy-start(bf16[128,128]{1,0:T(8,128)(2,1)} %get-tuple-element.15) | copy-start | bytes 98308
  65.0 0.8 %copy-start = (bf16[128,128]{1,0:T(8,128)(2,1)S(1)}, bf16[128,128]{1,0:T(8,128)(2,1)}, u32[]{:S(2)}) copy-start(bf16[128,128]{1,0:T(8,128)(2,1)} %get-tuple-element.16) | copy-start | bytes 98308
  65.8 0.7 copy-start.2
  66.5 0.7 copy-start.5
  67.2 0.6 copy-start.4
  67.8 0.7 copy-start.3

commit v2 on v1

v2 whole, which is shorter than its diff:
```python
import math

import numpy as np

import jax
import jax.numpy as jnp
from jax import lax
from jax.experimental import pallas as pl
from jax.experimental.pallas import tpu as pltpu
from jax.sharding import PartitionSpec as P

HD = 128
G = 8
BLK = 128
SUB = 8
PFX = 256
EPS = 1e-06
THETA = 1000000.0
Y = 4
Z = 16
GRP = 2 * Y
X = 4
JUMP = 4
NCTX = Y * Z * 2
ROWS = BLK * G
PROWS = 128
ALLR = ROWS + PROWS
KEYS = PFX + SUB * BLK
SCALE = HD ** (-0.5)
EXP2_SCALE = SCALE * math.log2(math.e)
MESH = pl.DeviceIdType.MESH
F32 = jnp.float32
BF16 = jnp.bfloat16


def prompt_order():
    p = np.arange(PFX)
    return (p // 64) * 64 + (p // 2 % Z) * 4 + (p // 32 % 2) * 2 + p % 2


def tables():
    freq = THETA ** (-(np.arange(HD // 2, dtype=np.float64) * 2.0) / HD)

    def pair(positions):
        angle = positions[:, None].astype(np.float64) * freq[None, :]
        cosine, sine = np.cos(angle), np.sin(angle)
        return np.stack(
            [np.concatenate([cosine, cosine], 1), np.concatenate([-sine, sine], 1)]
        ).astype(np.float32)

    offset = pair(np.arange(BLK))
    level = pair(np.arange(16) * BLK)
    prompt = pair(prompt_order())
    return offset, level, prompt


def norm(x):
    inverse = lax.rsqrt(jnp.mean(x * x, axis=-1, keepdims=True) + EPS)
    return x * inverse, inverse


def swap(x):
    return pltpu.roll(x, HD // 2, 1)


def rotate(x, c, s):
    return x * c + swap(x) * s


def unrotate(x, c, s):
    return x * c - swap(x) * s


def norm_back(grad, unit, inverse, gain, c, s):
    g = unrotate(grad, c, s)
    u = g * gain
    raw = (u - unit * jnp.mean(u * unit, axis=-1, keepdims=True)) * inverse
    return raw, jnp.sum(g * unit, axis=0, keepdims=True)


def nt(a, b):
    return lax.dot_general(a, b, (((1,), (1,)), ((), ())), preferred_element_type=F32)


def nn(a, b):
    return lax.dot_general(a, b, (((1,), (0,)), ((), ())), preferred_element_type=F32)


def kernel(
    q_hbm, k_hbm, v_hbm, o_hbm, do_hbm, pq_ref, pk_ref, pv_ref, po_ref, pdo_ref,
    gains_ref, par_ref, depth_ref, toff_hbm, tlev_ref, tpr_hbm,
    dq_ref, dk_ref, dv_ref, pdq_ref, pdk_ref, pdv_ref, gg_ref,
    q_ref, o_ref, do_ref, toff_ref, tpr_ref,
    kv, parw, zr, grp,
    qrot, qunit, qinv, dor, delta, krot, krott, kunit, kinv, ctab, stab, thr, eh, dsb, tot, dqt,
    qs, dos, scr, pscr, dn, vp,
    wterm, ownk, ownv, prx, mtx, mrx, pterm, rs1, rs2t, rs2, g1, g2,
    s_loc, s_kv, r_kv, s_par, r_par, s_zr, r_zr, s_ag2, r_ag2,
    s_p, r_p, s_m, r_m, s_rs1, r_rs1, s_rs2, r_rs2, s_g1, r_g1, s_g2, r_g2,
):
    me = lax.axis_index("ctx")
    hx = lax.axis_index("head")
    y = me // (2 * Z)
    z = lax.rem(me // 2, Z)
    c = lax.rem(me, 2)
    gi = y * 2 + c
    partner = me + 1 - 2 * c

    def at(offset):
        return lax.rem(me + (offset + NCTX), NCTX)

    def grp_dev(index):
        return ((index // 2) * Z + z) * 2 + lax.rem(index, 2)

    def z_dev(index):
        return (y * Z + index) * 2 + c

    def z_at(offset):
        return lax.rem(z + (offset + Z), Z)

    def copy(src, dst, ssem, rsem, device, head=None):
        where = {"ctx": device} if head is None else {"ctx": device, "head": head}
        return pltpu.make_async_remote_copy(
            src_ref=src, dst_ref=dst, send_sem=ssem, recv_sem=rsem,
            device_id=where, device_id_type=MESH,
        )

    barrier = pltpu.get_barrier_semaphore()

    def greet(device, head=None):
        where = {"ctx": device} if head is None else {"ctx": device, "head": head}
        pl.semaphore_signal(barrier, inc=1, device_id=where, device_id_type=MESH)

    for offset in (-7, -6, -5, -4, -3, -2, -1, 1, 2):
        greet(at(offset))
    for offset in range(1, JUMP + 1):
        greet(z_dev(z_at(offset)))
        greet(z_dev(z_at(-offset)))

    @pl.loop(1, GRP * X)
    def _(j):
        other = lax.rem(hx * GRP + gi + j, GRP * X)
        greet(grp_dev(lax.rem(other, GRP)), other // GRP)

    own = [
        pltpu.make_async_copy(k_hbm, kv.at[0, 0], s_loc.at[0]),
        pltpu.make_async_copy(v_hbm, kv.at[0, 1], s_loc.at[1]),
    ]
    later = [
        pltpu.make_async_copy(src, dst, s_loc.at[n])
        for n, src, dst in (
            (2, toff_hbm, toff_ref), (3, q_hbm, q_ref), (4, do_hbm, do_ref),
            (5, o_hbm, o_ref), (6, tpr_hbm, tpr_ref),
        )
    ]
    for cp in own + later:
        cp.start()
    parw[0] = jnp.full((1, HD), par_ref[0], jnp.int32)
    zr[z, 0] = pk_ref[...]
    zr[z, 1] = pv_ref[...]
    for cp in own:
        cp.wait()
    pl.semaphore_wait(barrier, 9 + 2 * JUMP + (GRP * X - 1))

    def kv_copy(op, n, src, dst, device):
        return copy(kv.at[src, n], kv.at[dst, n], s_kv.at[op, n], r_kv.at[dst, n], device)

    def kv_arrived(slot):
        for n in range(2):
            copy(kv.at[slot, n], kv.at[slot, n], s_kv.at[0, n], r_kv.at[slot, n], partner).wait_recv()

    sent = []

    def send(cp):
        cp.start()
        sent.append(cp)

    def zr_send(op, slot, to):
        send(copy(zr.at[slot], zr.at[slot], s_zr.at[op], r_zr.at[slot], z_dev(to)))

    def zr_arrived(slot):
        copy(zr.at[slot], zr.at[slot], s_zr.at[0], r_zr.at[slot], partner).wait_recv()

    for j in range(JUMP, 0, -1):
        zr_send(j, z, z_at(j))
        zr_send(JUMP + j, z, z_at(-j))
    for d in range(1, SUB):
        send(copy(parw.at[0], parw.at[d], s_par.at[d], r_par.at[d], at(d)))
    for n in range(2):
        send(kv_copy(0, n, 0, 2, at(2)))

    @pl.when(c == 0)
    def _():
        for n in range(2):
            kv_copy(1, n, 0, 1, partner).start()

    row16 = lax.broadcasted_iota(jnp.int32, (16, HD), 0)
    gain_q = gains_ref[0:1, :]
    gain_k = gains_ref[1:2, :]
    lane1 = lax.broadcasted_iota(jnp.int32, (1, HD), 1)
    level = (depth_ref[...] - lane1) >> 7

    def level_rows(lv):
        cl = jnp.zeros((1, HD), F32)
        sl = jnp.zeros((1, HD), F32)
        for n in range(1, SUB + 2):
            cl = jnp.where(lv == n, tlev_ref[0, n : n + 1, :], cl)
            sl = jnp.where(lv == n, tlev_ref[1, n : n + 1, :], sl)
        return cl, sl

    def block_tables(d, lv):
        cl, sl = level_rows(lv)
        co, so = toff_ref[0], toff_ref[1]
        ctab[d] = co * cl - so * sl
        stab[d] = so * cl + co * sl

    for cp in later:
        cp.wait()
    block_tables(0, level)

    @pl.loop(0, G)
    def _(g):
        lanes = pl.ds(pl.multiple_of(g * HD, HD), HD)
        rows = pl.ds(pl.multiple_of(g * BLK, BLK), BLK)
        unit, inverse = norm(q_ref[:, lanes].astype(F32))
        qunit[rows, :] = unit
        qinv[rows, :] = jnp.broadcast_to(inverse, (BLK, HD))
        qrot[rows, :] = rotate(unit * gain_q, ctab[0], stab[0]).astype(BF16)
        d = do_ref[:, lanes]
        dor[rows, :] = d
        prod = d.astype(F32) * o_ref[:, lanes].astype(F32)
        delta[:, lanes] = jnp.sum(prod.T, axis=0, keepdims=True)

    kv_arrived(2)
    for n in range(2):
        send(kv_copy(2, n, 2, 4, at(2)))
        send(kv_copy(3, n, 2, 3 - 2 * c, partner))
    for j in range(1, JUMP + 1):
        zr_arrived(z_at(-j))
        zr_send(2 * JUMP + j, z_at(-j), z_at(JUMP))
        zr_arrived(z_at(j))
        if j < JUMP:
            zr_send(3 * JUMP + j, z_at(j), z_at(-JUMP))

    def to_rows(ref):
        x = ref[...].astype(F32)
        for g in range(G):
            scr[2 * g : 2 * g + 2, :] = x[:, g * HD : (g + 1) * HD]
        return scr[0:16, :]

    pslot = gi * 32 + z * 2
    odd = lax.rem(row16, 2) == 1

    def prow(n):
        first = jnp.broadcast_to(tpr_ref[n, pl.ds(pslot, 1), :], (16, HD))
        second = jnp.broadcast_to(tpr_ref[n, pl.ds(pslot + 1, 1), :], (16, HD))
        return jnp.where(odd, second, first)

    pc16, ps16 = prow(0), prow(1)
    prest = pl.ds(ROWS + 16, PROWS - 16)
    punit, pinverse = norm(to_rows(pq_ref))
    qrot[ROWS : ROWS + 16, :] = rotate(punit * gain_q, pc16, ps16).astype(BF16)
    qrot[prest, :] = jnp.zeros((PROWS - 16, HD), BF16)
    pd = to_rows(pdo_ref)
    dor[ROWS : ROWS + 16, :] = pd.astype(BF16)
    dor[prest, :] = jnp.zeros((PROWS - 16, HD), BF16)
    pscr[...] = jnp.zeros((PROWS, HD), F32)
    pscr[0:16, :] = pd * to_rows(po_ref)
    delta[:, ROWS:] = jnp.sum(pscr[...].T, axis=0, keepdims=True)

    tot[...] = jnp.zeros((1, ALLR), F32)
    dqt[...] = jnp.zeros((HD, ALLR), F32)

    def attend(krows, vals, width, visible):
        s = nt(krot[krows, :], qrot[0:width, :])
        e = jnp.where(visible, jnp.exp2(s * EXP2_SCALE), 0.0)
        tot[:, 0:width] += jnp.sum(e, axis=0, keepdims=True)
        eh[krows, 0:width] = e.astype(BF16)
        dp = nt(vals, dor[0:width, :])
        ds = (e * (dp - delta[:, 0:width])).astype(BF16)
        dsb[krows, 0:width] = ds
        dqt[:, 0:width] += nn(krott[:, krows], ds)

    def key_block(d):
        rows = slice(PFX + d * BLK, PFX + (d + 1) * BLK)
        unit, inverse = norm(kv[d, 0].astype(F32))
        if d == 0:
            kinv[...] = jnp.broadcast_to(inverse, (BLK, HD))
        kunit[rows, :] = unit
        rot = rotate(unit * gain_k, ctab[d], stab[d])
        krot[rows, :] = rot.astype(BF16)
        krott[:, rows] = rot.T.astype(BF16)

    def wide(x):
        return jnp.concatenate([x] * G, axis=1)

    def window(first, count):
        for d in range(first, first + count):
            key_block(d)
        offs = lax.broadcasted_iota(jnp.int32, (BLK, ROWS), 0)
        visible = jnp.concatenate([offs <= thr[d] for d in range(first, first + count)], axis=0)
        vals = kv[first : first + count, 1].reshape(count * BLK, HD)
        attend(slice(PFX + first * BLK, PFX + (first + count) * BLK), vals, ROWS, visible)

    thr[0] = wide(lane1)
    window(0, 1)

    kv_arrived(4)
    for n in range(2):
        send(kv_copy(4, n, 4, 6, at(2)))
        send(kv_copy(5, n, 4, 5 - 2 * c, partner))

    for d in range(1, SUB):
        copy(parw.at[d], parw.at[d], s_par.at[d], r_par.at[d], partner).wait_recv()
    block = me + PFX // BLK
    current = jnp.full((1, HD), block, jnp.int32)
    seen = [jnp.zeros((1, HD), jnp.int32) for _ in range(SUB)]
    levels = [jnp.zeros((1, HD), jnp.int32) for _ in range(SUB)]
    above = [parw[d] for d in range(SUB)]
    for step in range(SUB + 1):
        branchy = current >= PFX // BLK
        upward = jnp.zeros((1, HD), jnp.int32)
        for d in range(SUB):
            match = (current == block - d) & branchy
            seen[d] = jnp.where(match, 1, seen[d])
            levels[d] = jnp.where(match, level - step, levels[d])
            upward = jnp.where(match, above[d], upward)
        current = jnp.where(branchy, upward, current)
    fork = current
    for d in range(1, SUB):
        thr[d] = jnp.where(wide(seen[d]) == 1, BLK, -1)
        block_tables(d, levels[d])
    thr_prompt = jnp.concatenate(
        [wide(BLK * (fork + 1) - 1), me * 2 + lax.rem(lane1, 2)], axis=1
    )

    kv_arrived(1)
    window(1, 2)

    kv_arrived(6)
    for n in range(2):
        send(kv_copy(6, n, 6, 7, at(1)))

    @pl.when(c == 1)
    def _():
        for n in range(2):
            kv_copy(7, n, 6, 5, partner).start()

    for j in range(JUMP + 1, 2 * JUMP + 1):
        zr_arrived(z_at(-j))
        if j < 2 * JUMP:
            zr_arrived(z_at(j))
    for n in range(2):
        for k in range(Z):
            dn[n * 32 + 2 * k : n * 32 + 2 * k + 2, :] = zr[k, n].astype(F32)
    grp[gi] = dn[...].astype(BF16)
    kv_arrived(3)
    for j in range(1, GRP):
        send(copy(grp.at[gi], grp.at[gi], s_ag2.at[j], r_ag2.at[gi], grp_dev(lax.rem(gi + j, GRP))))
    window(3, 2)
    kv_arrived(5)
    kv_arrived(7)
    window(5, 3)

    for j in range(1, GRP):
        slot = lax.rem(gi + j, GRP)
        copy(grp.at[slot], grp.at[slot], s_ag2.at[j], r_ag2.at[slot], partner).wait_recv()
    pcos, psin = tpr_ref[0], tpr_ref[1]
    pk_all = jnp.concatenate([grp[n, 0:32, :] for n in range(GRP)], axis=0).astype(F32)
    pv_all = jnp.concatenate([grp[n, 32:64, :] for n in range(GRP)], axis=0)
    pkunit, _ = norm(pk_all)
    rot = rotate(pkunit * gain_k, pcos, psin)
    krot[0:PFX, :] = rot.astype(BF16)
    krott[:, 0:PFX] = rot.T.astype(BF16)
    kunit[0:PFX, :] = pkunit
    p_key = lax.broadcasted_iota(jnp.int32, (PFX, ALLR), 0)
    t_key = ((p_key >> 6) << 6) + (((p_key >> 1) & 15) << 2) + (((p_key >> 5) & 1) << 1) + (p_key & 1)
    attend(slice(0, PFX), pv_all, ALLR, t_key <= thr_prompt)

    tot[...] = 1.0 / tot[...]
    for g in range(G + 1):
        rows = slice(g * BLK, (g + 1) * BLK)
        column = jnp.broadcast_to(tot[:, rows], (BLK, BLK)).T
        qs[rows, :] = (qrot[rows, :].astype(F32) * column).astype(BF16)
        dos[rows, :] = (dor[rows, :].astype(F32) * column).astype(BF16)

    def key_grads(krows, width):
        dk = nn(dsb[krows, 0:width], qs[0:width, :]) * SCALE
        return dk, nn(eh[krows, 0:width], dos[0:width, :])

    dk, dv = key_grads(slice(0, PFX), ALLR)
    for n in range(GRP):
        pterm[n, 0:32, :] = dk[n * 32 : (n + 1) * 32].astype(BF16)
        pterm[n, 32:64, :] = dv[n * 32 : (n + 1) * 32].astype(BF16)
    gk = jnp.sum(unrotate(dk, pcos, psin) * kunit[0:PFX, :], axis=0, keepdims=True)
    for j in range(1, GRP):
        other = lax.rem(gi + j, GRP)
        send(copy(pterm.at[other], rs1.at[gi], s_rs1.at[j], r_rs1.at[gi], grp_dev(other)))

    dk, dv = key_grads(slice(PFX, KEYS), ROWS)
    for d in range(SUB - 1, -1, -1):
        rows = slice(d * BLK, (d + 1) * BLK)
        if d:
            wterm[d, 0] = dk[rows].astype(BF16)
            wterm[d, 1] = dv[rows].astype(BF16)
        else:
            ownk[...] = dk[rows]
            ownv[...] = dv[rows]
        g_part = unrotate(dk[rows], ctab[d], stab[d]) * kunit[PFX + d * BLK : PFX + (d + 1) * BLK, :]
        gk = gk + jnp.sum(g_part, axis=0, keepdims=True)
    for n in range(2):
        send(copy(wterm.at[7, n], prx.at[3, n], s_p.at[3, n], r_p.at[3, n], at(-1)))
    for slot in (2, 1, 0):
        for n in range(2):
            send(copy(wterm.at[2 * slot + 1, n], prx.at[slot, n], s_p.at[slot, n], r_p.at[slot, n], partner))

    gq = jnp.zeros((1, HD), F32)
    for g in range(G):
        rows = slice(g * BLK, (g + 1) * BLK)
        grad = (dqt[:, rows] * (tot[:, rows] * SCALE)).T
        raw, part = norm_back(grad, qunit[rows, :], qinv[rows, :], gain_q, ctab[0], stab[0])
        dq_ref[:, rows] = raw.astype(BF16)
        gq = gq + part
    grad = (dqt[:, ROWS:] * (tot[:, ROWS:] * SCALE)).T[0:16]
    raw, part = norm_back(grad, punit, pinverse, gain_q, pc16, ps16)
    gq = gq + part
    row8 = lax.broadcasted_iota(jnp.int32, (8, HD), 0)
    g1[z] = jnp.where(row8 == 0, gq, jnp.where(row8 == 1, gk, 0.0))
    scr[...] = raw
    for g in range(G):
        pdq_ref[:, g * HD : (g + 1) * HD] = scr[2 * g : 2 * g + 2, :].astype(BF16)

    @pl.loop(1, Z)
    def _(j):
        copy(g1.at[z], g1.at[z], s_g1.at[j], r_g1.at[z], z_dev(lax.rem(z + j, Z))).start()

    def p_arrived(slot, n):
        copy(prx.at[slot, n], prx.at[slot, n], s_p.at[slot, n], r_p.at[slot, n], partner).wait_recv()

    def m_arrived(k, n):
        copy(mrx.at[k, n], mrx.at[k, n], s_m.at[k, n], r_m.at[k, n], partner).wait_recv()

    def step_down(k):
        for n in range(2):
            if k < 3:
                m_arrived(k, n)
            value = wterm[2 * k, n].astype(F32) + prx[k - c, n].astype(F32)
            if k == 3:
                value = value + jnp.where(c == 1, prx[3, n].astype(F32), 0.0)
            else:
                value = value + mrx[k, n].astype(F32)
            mtx[k - 1, n] = value.astype(BF16)
        for n in range(2):
            send(copy(mtx.at[k - 1, n], mrx.at[k - 1, n], s_m.at[k - 1, n], r_m.at[k - 1, n], at(-2)))

    for slot in range(4):
        for n in range(2):
            p_arrived(slot, n)
    step_down(3)

    for j in range(1, GRP):
        slot = lax.rem(gi + j, GRP)
        copy(rs1.at[slot], rs1.at[slot], s_rs1.at[j], r_rs1.at[slot], partner).wait_recv()
    rs1[gi] = pterm[gi]
    total = rs1[0].astype(F32)
    for n in range(1, GRP):
        total = total + rs1[n].astype(F32)
    dn[...] = total
    for n in range(2):
        for k in range(Z):
            rs2t[k, n] = dn[n * 32 + 2 * k : n * 32 + 2 * k + 2, :]
    rs2[z] = rs2t[z]

    @pl.loop(1, Z)
    def _(j):
        other = lax.rem(z + j, Z)
        copy(rs2t.at[other], rs2.at[z], s_rs2.at[j], r_rs2.at[z], z_dev(other)).start()

    step_down(2)

    @pl.loop(1, Z)
    def _(j):
        slot = lax.rem(z + j, Z)
        copy(g1.at[slot], g1.at[slot], s_g1.at[j], r_g1.at[slot], partner).wait_recv()

    total = g1[0]
    for n in range(1, Z):
        total = total + g1[n]
    xg = hx * GRP + gi
    g2[xg] = total

    @pl.loop(1, GRP * X)
    def _(j):
        other = lax.rem(xg + j, GRP * X)
        copy(
            g2.at[xg], g2.at[xg], s_g2.at[j], r_g2.at[xg], grp_dev(lax.rem(other, GRP)), other // GRP
        ).start()

    step_down(1)

    for n, total_ref in ((0, ownk), (1, ownv)):
        m_arrived(0, n)
        total_ref[...] += mrx[0, n].astype(F32)

        @pl.when(c == 0)
        def _():
            total_ref[...] += prx[0, n].astype(F32)

    raw, _ = norm_back(
        ownk[...], kunit[PFX : PFX + BLK, :], kinv[...], gain_k, ctab[0], stab[0]
    )
    dk_ref[...] = raw.astype(BF16)
    dv_ref[...] = ownv[...].astype(BF16)

    @pl.loop(1, Z)
    def _(j):
        slot = lax.rem(z + j, Z)
        copy(rs2.at[slot], rs2.at[slot], s_rs2.at[j], r_rs2.at[slot], partner).wait_recv()

    ptk, ptv = rs2[0, 0], rs2[0, 1]
    for n in range(1, Z):
        ptk = ptk + rs2[n, 0]
        ptv = ptv + rs2[n, 1]
    unit2, inverse2 = norm(pk_ref[...].astype(F32))
    raw, _ = norm_back(ptk, unit2, inverse2, gain_k, pc16[0:2], ps16[0:2])
    pdk_ref[...] = raw.astype(BF16)
    pdv_ref[...] = ptv.astype(BF16)

    @pl.loop(1, GRP * X)
    def _(j):
        slot = lax.rem(xg + j, GRP * X)
        copy(g2.at[slot], g2.at[slot], s_g2.at[j], r_g2.at[slot], partner).wait_recv()

    total = g2[0]
    for n in range(1, GRP * X):
        total = total + g2[n]
    count = (NCTX * (BLK + 2)) * X
    factor = jnp.where(row8 == 0, (count * G) ** (-0.5), count ** (-0.5))
    gg_ref[...] = (total * factor)[0:2]

    for cp in sent:
        cp.wait_send()

    @pl.when(c == 0)
    def _():
        for n in range(2):
            kv_copy(1, n, 0, 1, partner).wait_send()

    @pl.when(c == 1)
    def _():
        for n in range(2):
            kv_copy(7, n, 6, 5, partner).wait_send()

    @pl.loop(1, Z)
    def _(j):
        copy(rs2t.at[z], rs2.at[z], s_rs2.at[j], r_rs2.at[z], partner).wait_send()
        copy(g1.at[z], g1.at[z], s_g1.at[j], r_g1.at[z], partner).wait_send()

    @pl.loop(1, GRP * X)
    def _(j):
        copy(g2.at[0], g2.at[0], s_g2.at[j], r_g2.at[0], partner).wait_send()


def per_device(
    branch_q, branch_k, branch_v, branch_o, branch_dout,
    prompt_q, prompt_k, prompt_v, prompt_o, prompt_dout, gains, parents, depth,
):
    offset, level, prompt = tables()
    vmem = pl.BlockSpec(memory_space=pltpu.VMEM)
    hbm = pl.BlockSpec(memory_space=pl.ANY)
    smem = pl.BlockSpec(memory_space=pltpu.SMEM)
    dma = pltpu.SemaphoreType.DMA
    vm = pltpu.VMEM
    outs = pl.pallas_call(
        kernel,
        out_shape=(
            jax.ShapeDtypeStruct((BLK, G * HD), BF16),
            jax.ShapeDtypeStruct((BLK, HD), BF16),
            jax.ShapeDtypeStruct((BLK, HD), BF16),
            jax.ShapeDtypeStruct((2, G * HD), BF16),
            jax.ShapeDtypeStruct((2, HD), BF16),
            jax.ShapeDtypeStruct((2, HD), BF16),
            jax.ShapeDtypeStruct((2, HD), F32),
        ),
        in_specs=[hbm] * 5 + [vmem] * 6 + [smem, vmem, hbm, vmem, hbm],
        out_specs=(vmem,) * 7,
        scratch_shapes=[
            vm((BLK, G * HD), BF16),
            vm((BLK, G * HD), BF16),
            vm((BLK, G * HD), BF16),
            vm((2, BLK, HD), F32),
            vm((2, PFX, HD), F32),
            vm((SUB, 2, BLK, HD), BF16),
            vm((SUB, 1, HD), jnp.int32),
            vm((Z, 2, 2, HD), BF16),
            vm((GRP, 64, HD), BF16),
            vm((ALLR, HD), BF16),
            vm((ROWS, HD), F32),
            vm((ROWS, HD), F32),
            vm((ALLR, HD), BF16),
            vm((1, ALLR), F32),
            vm((KEYS, HD), BF16),
            vm((HD, KEYS), BF16),
            vm((KEYS, HD), F32),
            vm((BLK, HD), F32),
            vm((SUB, BLK, HD), F32),
            vm((SUB, BLK, HD), F32),
            vm((SUB, 1, ROWS), jnp.int32),
            vm((KEYS, ALLR), BF16),
            vm((KEYS, ALLR), BF16),
            vm((1, ALLR), F32),
            vm((HD, ALLR), F32),
            vm((ALLR, HD), BF16),
            vm((ALLR, HD), BF16),
            vm((16, HD), F32),
            vm((PROWS, HD), F32),
            vm((64, HD), F32),
            vm((PFX, HD), BF16),
            vm((SUB, 2, BLK, HD), BF16),
            vm((BLK, HD), F32),
            vm((BLK, HD), F32),
            vm((4, 2, BLK, HD), BF16),
            vm((3, 2, BLK, HD), BF16),
            vm((3, 2, BLK, HD), BF16),
            vm((GRP, 64, HD), BF16),
            vm((GRP, 64, HD), BF16),
            vm((Z, 2, 2, HD), F32),
            vm((Z, 2, 2, HD), F32),
            vm((Z, 8, HD), F32),
            vm((GRP * X, 8, HD), F32),
            dma((7,)),
            dma((8, 2)), dma((SUB, 2)),
            dma((SUB,)), dma((SUB,)),
            dma((4 * JUMP + 1,)), dma((Z,)),
            dma((GRP,)), dma((GRP,)),
            dma((4, 2)), dma((4, 2)),
            dma((3, 2)), dma((3, 2)),
            dma((GRP,)), dma((GRP,)),
            dma((Z,)), dma((Z,)),
            dma((Z,)), dma((Z,)),
            dma((GRP * X,)), dma((GRP * X,)),
        ],
        compiler_params=pltpu.CompilerParams(
            collective_id=0, has_side_effects=True, vmem_limit_bytes=60 * 1024 * 1024
        ),
        name="tree_back",
    )(
        branch_q[:, 0], branch_k[:, 0], branch_v[:, 0], branch_o[:, 0], branch_dout[:, 0],
        prompt_q[:, 0], prompt_k[:, 0], prompt_v[:, 0], prompt_o[:, 0], prompt_dout[:, 0],
        gains, parents, depth.reshape(1, BLK),
        jnp.asarray(offset), jnp.asarray(level), jnp.asarray(prompt),
    )
    dq, dk, dv, pdq, pdk, pdv, gain_grads = outs
    return (
        dq[:, None], dk[:, None], dv[:, None], pdq[:, None], pdk[:, None], pdv[:, None], gain_grads,
    )


def solution(mesh):
    tok = P("ctx", "head", None)
    return jax.shard_map(
        per_device,
        mesh=mesh,
        in_specs=(tok,) * 10 + (P(), P("ctx"), P("ctx")),
        out_specs=(tok,) * 6 + (P(),),
        check_vma=False,
    )
```

time: 69.3 us -> 59.8 us (0.86)
  Pallas kernels: 62.1 us -> 52.5 us
    pallas_call x1, Pallas kernels: 62.1 us -> 52.5 us  [per_device(): pl.pallas_call(kernel, out_shape=(jax.ShapeDtypeStruct((BLK, G * HD), BF1...]
where the time goes in v2:
time: 59.8 us; the launch traced here: 59.5 us
  Pallas kernels  52.5 us (88%)
  local copies, waits for them, and re-layouts  5.67 us (9%)
  between operations  1.31 us (2%)
    pallas_call x1, Pallas kernels, per_device(): pl.pallas_call(kernel, out_shape=(jax.ShapeDtypeStruct((BLK, G * HD), BF1...  52.5 us
    unnamed x19, local copies, waits for them, and re-layouts  5.67 us

profile of v2, /device:TPU:1, one launch (start us, length us, event | category | flops | bytes accessed | tf_op | source)
XLA Modules:
  0.0 59.5 jit_solution(3831346017076565548)
XLA Ops:
  1.3 52.5 %tree_back.1 = (bf16[128,1024]{1,0:T(8,128)(2,1)}, bf16[128,128]{1,0:T(8,128)(2,1)}, bf16[128,128]{1,0:T(8,128)(2,1)}, bf16[2,1024]{1,0:T(2,128)(2,1)}, bf16[2,1...) custom-call(bf16[128,1024]{1,0:T(8,128)(2,1)} %bitcast.18, bf16[128,128]{1,0:T(8,128)(2,1)} %bitcast.21, ...), custom_call_target="tpu_custom_call" | custom-call | tf_op jit(solution)/shard_map/tree_back/pallas_call | solution.py:574
  53.8 0.0 copy-start.1
  53.8 1.7 %copy.31 = bf16[128,1,1024]{2,0,1:T(8,128)(2,1)} copy(bf16[128,1,1024]{2,0,1:T(8,128)(2,1)} %bitcast.17) | data formatting | bytes 524288
  55.5 0.0 copy-done.1
  55.5 0.0 copy-start
  55.5 0.6 %copy.32 = bf16[128,1,128]{2,0,1:T(8,128)(2,1)} copy(bf16[128,1,128]{2,0,1:T(8,128)(2,1)S(1)} %bitcast.24) | data formatting | bytes 65536
  56.1 0.2 copy-done
  56.3 0.0 copy-start.2
  56.3 0.6 %copy.33 = bf16[128,1,128]{2,0,1:T(8,128)(2,1)} copy(bf16[128,1,128]{2,0,1:T(8,128)(2,1)S(1)} %bitcast.23) | data formatting | bytes 65536
  56.9 0.1 copy-done.2
  56.9 0.0 copy-start.5
  57.0 0.6 copy.34
  57.5 0.1 copy-done.5
  57.6 0.0 copy-start.4
  57.6 0.5 copy.35
  58.1 0.1 copy-done.4
  58.3 0.0 copy-start.3
  58.3 0.5 copy.36
  58.8 0.2 copy-done.3
  58.9 0.6 copy.37
Async XLA Ops:
  53.8 1.7 %copy-start.1 = (bf16[128,128]{1,0:T(8,128)(2,1)S(1)}, bf16[128,128]{1,0:T(8,128)(2,1)}, u32[]{:S(2)}) copy-start(bf16[128,128]{1,0:T(8,128)(2,1)} %get-tuple-element.15) | copy-start | bytes 98308
  55.5 0.8 %copy-start = (bf16[128,128]{1,0:T(8,128)(2,1)S(1)}, bf16[128,128]{1,0:T(8,128)(2,1)}, u32[]{:S(2)}) copy-start(bf16[128,128]{1,0:T(8,128)(2,1)} %get-tuple-element.16) | copy-start | bytes 98308
  56.3 0.7 %copy-start.2 = (bf16[2,1024]{1,0:T(2,128)(2,1)S(1)}, bf16[2,1024]{1,0:T(2,128)(2,1)}, u32[]{:S(2)}) copy-start(bf16[2,1024]{1,0:T(2,128)(2,1)} %get-tuple-element.17) | copy-start | bytes 12292
  56.9 0.7 %copy-start.5 = (bf16[2,128]{1,0:T(2,128)(2,1)S(1)}, bf16[2,128]{1,0:T(2,128)(2,1)}, u32[]{:S(2)}) copy-start(bf16[2,128]{1,0:T(2,128)(2,1)} %get-tuple-element.18) | copy-start | bytes 1540
  57.6 0.6 %copy-start.4 = (bf16[2,128]{1,0:T(2,128)(2,1)S(1)}, bf16[2,128]{1,0:T(2,128)(2,1)}, u32[]{:S(2)}) copy-start(bf16[2,128]{1,0:T(2,128)(2,1)} %get-tuple-element.19) | copy-start | bytes 1540
  58.3 0.7 %copy-start.3 = (f32[2,128]{1,0:T(2,128)S(1)}, f32[2,128]{1,0:T(2,128)}, u32[]{:S(2)}) copy-start(f32[2,128]{1,0:T(2,128)} %get-tuple-element.34) | copy-start | bytes 3076

commit v3 on v2

--- a/solution.py
+++ b/solution.py
@@ -87,13 +87,13 @@
 
 
 def kernel(
-    q_hbm, k_hbm, v_hbm, o_hbm, do_hbm, pq_ref, pk_ref, pv_ref, po_ref, pdo_ref,
-    gains_ref, par_ref, depth_ref, toff_hbm, tlev_ref, tpr_hbm,
-    dq_ref, dk_ref, dv_ref, pdq_ref, pdk_ref, pdv_ref, gg_ref,
-    q_ref, o_ref, do_ref, toff_ref, tpr_ref,
+    q_hbm, k_hbm, v_hbm, o_hbm, do_hbm, pq_hbm, pk_hbm, pv_hbm, po_hbm, pdo_hbm,
+    gains_hbm, par_hbm, depth_hbm, tab_hbm,
+    dq_hbm, dk_ref, dv_ref, pdq_ref, pdk_ref, pdv_ref, gg_ref,
+    qod, pqod, tab, dq_ref, gains_ref, par_ref, depth_ref,
     kv, parw, zr, grp,
     qrot, qunit, qinv, dor, delta, krot, krott, kunit, kinv, ctab, stab, thr, eh, dsb, tot, dqt,
-    qs, dos, scr, pscr, dn, vp,
+    qs, dos, scr, pscr, dn,
     wterm, ownk, ownv, prx, mtx, mrx, pterm, rs1, rs2t, rs2, g1, g2,
     s_loc, s_kv, r_kv, s_par, r_par, s_zr, r_zr, s_ag2, r_ag2,
     s_p, r_p, s_m, r_m, s_rs1, r_rs1, s_rs2, r_rs2, s_g1, r_g1, s_g2, r_g2,
@@ -142,59 +142,72 @@
         other = lax.rem(hx * GRP + gi + j, GRP * X)
         greet(grp_dev(lax.rem(other, GRP)), other // GRP)
 
-    own = [
-        pltpu.make_async_copy(k_hbm, kv.at[0, 0], s_loc.at[0]),
-        pltpu.make_async_copy(v_hbm, kv.at[0, 1], s_loc.at[1]),
-    ]
-    later = [
-        pltpu.make_async_copy(src, dst, s_loc.at[n])
-        for n, src, dst in (
-            (2, toff_hbm, toff_ref), (3, q_hbm, q_ref), (4, do_hbm, do_ref),
-            (5, o_hbm, o_ref), (6, tpr_hbm, tpr_ref),
-        )
-    ]
-    for cp in own + later:
+    def fetch(n, src, dst):
+        cp = pltpu.make_async_copy(src, dst, s_loc.at[n])
         cp.start()
-    parw[0] = jnp.full((1, HD), par_ref[0], jnp.int32)
-    zr[z, 0] = pk_ref[...]
-    zr[z, 1] = pv_ref[...]
-    for cp in own:
-        cp.wait()
+        return cp
+
+    par_in = fetch(0, par_hbm, par_ref)
+    fetch(1, pk_hbm, zr.at[z, 0])
+    fetch(1, pv_hbm, zr.at[z, 1])
+    fetch(2, k_hbm, kv.at[0, 0])
+    fetch(2, v_hbm, kv.at[0, 1])
+    later = [fetch(3, gains_hbm, gains_ref), fetch(4, depth_hbm, depth_ref), fetch(5, tab_hbm, tab)]
+    for n, (big, small) in enumerate(((q_hbm, pq_hbm), (o_hbm, po_hbm), (do_hbm, pdo_hbm))):
+        fetch(6, big, qod.at[n])
+        fetch(7, small, pqod.at[n])
+    toff_ref = tab.at[:, 0:BLK]
+    tlev_ref = tab.at[:, BLK : BLK + 16]
+    tpr_ref = tab.at[:, BLK + 16 :]
+
+    def fetched(n, ref):
+        pltpu.make_async_copy(ref, ref, s_loc.at[n]).wait()
+
+    par_in.wait()
+    fetched(1, zr.at[z])
+    fetched(2, kv.at[0])
+    parw[0] = jnp.broadcast_to(par_ref[...], (1, HD))
     pl.semaphore_wait(barrier, 9 + 2 * JUMP + (GRP * X - 1))
 
-    def kv_copy(op, n, src, dst, device):
-        return copy(kv.at[src, n], kv.at[dst, n], s_kv.at[op, n], r_kv.at[dst, n], device)
-
-    def kv_arrived(slot):
-        for n in range(2):
-            copy(kv.at[slot, n], kv.at[slot, n], s_kv.at[0, n], r_kv.at[slot, n], partner).wait_recv()
-
-    sent = []
+    def kv_copy(n, src, dst, device):
+        return copy(kv.at[src, n], kv.at[dst, n], s_kv.at[0], r_kv.at[dst, n], device)
+
+    def kv_arrived(slot, halves=(0, 1)):
+        for n in halves:
+            copy(kv.at[slot, n], kv.at[slot, n], s_kv.at[0], r_kv.at[slot, n], partner).wait_recv()
 
     def send(cp):
         cp.start()
-        sent.append(cp)
-
-    def zr_send(op, slot, to):
-        send(copy(zr.at[slot], zr.at[slot], s_zr.at[op], r_zr.at[slot], z_dev(to)))
-
-    def zr_arrived(slot):
-        copy(zr.at[slot], zr.at[slot], s_zr.at[0], r_zr.at[slot], partner).wait_recv()
+
+    def sum_wait(ref, count, sem):
+        part = ref.at[pl.ds(0, count)]
+        copy(part, part, sem, sem, partner).wait_recv()
+
+    def sent(ref, count, sem):
+        part = ref.at[pl.ds(0, count)]
+        copy(part, part, sem, sem, partner).wait_send()
+
+    def zr_send(far, slot, to):
+        copy(zr.at[slot], zr.at[slot], s_zr.at[0], r_zr.at[far], z_dev(to)).start()
 
     for j in range(JUMP, 0, -1):
-        zr_send(j, z, z_at(j))
-        zr_send(JUMP + j, z, z_at(-j))
+        zr_send(0, z, z_at(j))
+        zr_send(0, z, z_at(-j))
     for d in range(1, SUB):
-        send(copy(parw.at[0], parw.at[d], s_par.at[d], r_par.at[d], at(d)))
-    for n in range(2):
-        send(kv_copy(0, n, 0, 2, at(2)))
+        send(copy(parw.at[0], parw.at[d], s_par.at[0], r_par.at[0], at(d)))
+    for n in range(2):
+        send(kv_copy(n, 0, 2, at(2)))
 
     @pl.when(c == 0)
     def _():
         for n in range(2):
-            kv_copy(1, n, 0, 1, partner).start()
+            kv_copy(n, 0, 1, partner).start()
 
     row16 = lax.broadcasted_iota(jnp.int32, (16, HD), 0)
+    for cp in later:
+        cp.wait()
+    fetched(6, qod)
+    fetched(7, pqod)
     gain_q = gains_ref[0:1, :]
     gain_k = gains_ref[1:2, :]
     lane1 = lax.broadcasted_iota(jnp.int32, (1, HD), 1)
@@ -214,36 +227,33 @@
         ctab[d] = co * cl - so * sl
         stab[d] = so * cl + co * sl
 
-    for cp in later:
-        cp.wait()
     block_tables(0, level)
 
     @pl.loop(0, G)
     def _(g):
         lanes = pl.ds(pl.multiple_of(g * HD, HD), HD)
         rows = pl.ds(pl.multiple_of(g * BLK, BLK), BLK)
-        unit, inverse = norm(q_ref[:, lanes].astype(F32))
+        unit, inverse = norm(qod[0, :, lanes].astype(F32))
         qunit[rows, :] = unit
         qinv[rows, :] = jnp.broadcast_to(inverse, (BLK, HD))
         qrot[rows, :] = rotate(unit * gain_q, ctab[0], stab[0]).astype(BF16)
-        d = do_ref[:, lanes]
+        d = qod[2, :, lanes]
         dor[rows, :] = d
-        prod = d.astype(F32) * o_ref[:, lanes].astype(F32)
+        prod = d.astype(F32) * qod[1, :, lanes].astype(F32)
         delta[:, lanes] = jnp.sum(prod.T, axis=0, keepdims=True)
 
-    kv_arrived(2)
-    for n in range(2):
-        send(kv_copy(2, n, 2, 4, at(2)))
-        send(kv_copy(3, n, 2, 3 - 2 * c, partner))
+    for n in range(2):
+        kv_arrived(2, (n,))
+        send(kv_copy(n, 2, 4, at(2)))
+        send(kv_copy(n, 2, 3 - 2 * c, partner))
+    sum_wait(zr, 2 * JUMP, r_zr.at[0])
     for j in range(1, JUMP + 1):
-        zr_arrived(z_at(-j))
-        zr_send(2 * JUMP + j, z_at(-j), z_at(JUMP))
-        zr_arrived(z_at(j))
+        zr_send(1, z_at(-j), z_at(JUMP))
         if j < JUMP:
-            zr_send(3 * JUMP + j, z_at(j), z_at(-JUMP))
-
-    def to_rows(ref):
-        x = ref[...].astype(F32)
+            zr_send(1, z_at(j), z_at(-JUMP))
+
+    def to_rows(n):
+        x = pqod[n].astype(F32)
         for g in range(G):
             scr[2 * g : 2 * g + 2, :] = x[:, g * HD : (g + 1) * HD]
         return scr[0:16, :]
@@ -258,14 +268,14 @@
 
     pc16, ps16 = prow(0), prow(1)
     prest = pl.ds(ROWS + 16, PROWS - 16)
-    punit, pinverse = norm(to_rows(pq_ref))
+    punit, pinverse = norm(to_rows(0))
     qrot[ROWS : ROWS + 16, :] = rotate(punit * gain_q, pc16, ps16).astype(BF16)
     qrot[prest, :] = jnp.zeros((PROWS - 16, HD), BF16)
-    pd = to_rows(pdo_ref)
+    pd = to_rows(2)
     dor[ROWS : ROWS + 16, :] = pd.astype(BF16)
     dor[prest, :] = jnp.zeros((PROWS - 16, HD), BF16)
     pscr[...] = jnp.zeros((PROWS, HD), F32)
-    pscr[0:16, :] = pd * to_rows(po_ref)
+    pscr[0:16, :] = pd * to_rows(1)
     delta[:, ROWS:] = jnp.sum(pscr[...].T, axis=0, keepdims=True)
 
     tot[...] = jnp.zeros((1, ALLR), F32)
@@ -276,7 +286,7 @@
         e = jnp.where(visible, jnp.exp2(s * EXP2_SCALE), 0.0)
         tot[:, 0:width] += jnp.sum(e, axis=0, keepdims=True)
         eh[krows, 0:width] = e.astype(BF16)
-        dp = nt(vals, dor[0:width, :])
+        dp = nt(vals(), dor[0:width, :])
         ds = (e * (dp - delta[:, 0:width])).astype(BF16)
         dsb[krows, 0:width] = ds
         dqt[:, 0:width] += nn(krott[:, krows], ds)
@@ -299,19 +309,17 @@
             key_block(d)
         offs = lax.broadcasted_iota(jnp.int32, (BLK, ROWS), 0)
         visible = jnp.concatenate([offs <= thr[d] for d in range(first, first + count)], axis=0)
-        vals = kv[first : first + count, 1].reshape(count * BLK, HD)
-        attend(slice(PFX + first * BLK, PFX + (first + count) * BLK), vals, ROWS, visible)
+        attend(slice(PFX + first * BLK, PFX + (first + count) * BLK), lambda: kv[first : first + count, 1].reshape(count * BLK, HD), ROWS, visible)
 
     thr[0] = wide(lane1)
     window(0, 1)
 
-    kv_arrived(4)
-    for n in range(2):
-        send(kv_copy(4, n, 4, 6, at(2)))
-        send(kv_copy(5, n, 4, 5 - 2 * c, partner))
-
-    for d in range(1, SUB):
-        copy(parw.at[d], parw.at[d], s_par.at[d], r_par.at[d], partner).wait_recv()
+    for n in range(2):
+        kv_arrived(4, (n,))
+        send(kv_copy(n, 4, 6, at(2)))
+        send(kv_copy(n, 4, 5 - 2 * c, partner))
+
+    sum_wait(parw, SUB - 1, r_par.at[0])
     block = me + PFX // BLK
     current = jnp.full((1, HD), block, jnp.int32)
     seen = [jnp.zeros((1, HD), jnp.int32) for _ in range(SUB)]
@@ -337,37 +345,39 @@
     kv_arrived(1)
     window(1, 2)
 
-    kv_arrived(6)
-    for n in range(2):
-        send(kv_copy(6, n, 6, 7, at(1)))
-
-    @pl.when(c == 1)
-    def _():
-        for n in range(2):
-            kv_copy(7, n, 6, 5, partner).start()
-
-    for j in range(JUMP + 1, 2 * JUMP + 1):
-        zr_arrived(z_at(-j))
-        if j < 2 * JUMP:
-            zr_arrived(z_at(j))
+    def last_hop(n):
+        kv_arrived(6, (n,))
+        send(kv_copy(n, 6, 7, at(1)))
+
+        @pl.when(c == 1)
+        def _():
+            kv_copy(n, 6, 5, partner).start()
+
+    for n in range(2):
+        last_hop(n)
+
+    sum_wait(zr, 2 * JUMP - 1, r_zr.at[1])
     for n in range(2):
         for k in range(Z):
             dn[n * 32 + 2 * k : n * 32 + 2 * k + 2, :] = zr[k, n].astype(F32)
-    grp[gi] = dn[...].astype(BF16)
+    grp[0, gi] = dn[0:32, :].astype(BF16)
+    grp[1, gi] = dn[32:64, :].astype(BF16)
     kv_arrived(3)
-    for j in range(1, GRP):
-        send(copy(grp.at[gi], grp.at[gi], s_ag2.at[j], r_ag2.at[gi], grp_dev(lax.rem(gi + j, GRP))))
+    for n in range(2):
+        for j in range(1, GRP):
+            other = grp_dev(lax.rem(gi + j, GRP))
+            send(copy(grp.at[n, gi], grp.at[n, gi], s_ag2.at[n], r_ag2.at[n], other))
     window(3, 2)
     kv_arrived(5)
     kv_arrived(7)
     window(5, 3)
 
-    for j in range(1, GRP):
-        slot = lax.rem(gi + j, GRP)
-        copy(grp.at[slot], grp.at[slot], s_ag2.at[j], r_ag2.at[slot], partner).wait_recv()
+    def grp_arrived(n):
+        sum_wait(grp.at[n], GRP - 1, r_ag2.at[n])
+
+    grp_arrived(0)
     pcos, psin = tpr_ref[0], tpr_ref[1]
-    pk_all = jnp.concatenate([grp[n, 0:32, :] for n in range(GRP)], axis=0).astype(F32)
-    pv_all = jnp.concatenate([grp[n, 32:64, :] for n in range(GRP)], axis=0)
+    pk_all = grp[0].reshape(PFX, HD).astype(F32)
     pkunit, _ = norm(pk_all)
     rot = rotate(pkunit * gain_k, pcos, psin)
     krot[0:PFX, :] = rot.astype(BF16)
@@ -375,7 +385,12 @@
     kunit[0:PFX, :] = pkunit
     p_key = lax.broadcasted_iota(jnp.int32, (PFX, ALLR), 0)
     t_key = ((p_key >> 6) << 6) + (((p_key >> 1) & 15) << 2) + (((p_key >> 5) & 1) << 1) + (p_key & 1)
-    attend(slice(0, PFX), pv_all, ALLR, t_key <= thr_prompt)
+
+    def prompt_values():
+        grp_arrived(1)
+        return grp[1].reshape(PFX, HD)
+
+    attend(slice(0, PFX), prompt_values, ALLR, t_key <= thr_prompt)
 
     tot[...] = 1.0 / tot[...]
     for g in range(G + 1):
@@ -395,7 +410,7 @@
     gk = jnp.sum(unrotate(dk, pcos, psin) * kunit[0:PFX, :], axis=0, keepdims=True)
     for j in range(1, GRP):
         other = lax.rem(gi + j, GRP)
-        send(copy(pterm.at[other], rs1.at[gi], s_rs1.at[j], r_rs1.at[gi], grp_dev(other)))
+        send(copy(pterm.at[other], rs1.at[gi], s_rs1.at[0], r_rs1.at[0], grp_dev(other)))
 
     dk, dv = key_grads(slice(PFX, KEYS), ROWS)
     for d in range(SUB - 1, -1, -1):
@@ -409,10 +424,10 @@
         g_part = unrotate(dk[rows], ctab[d], stab[d]) * kunit[PFX + d * BLK : PFX + (d + 1) * BLK, :]
         gk = gk + jnp.sum(g_part, axis=0, keepdims=True)
     for n in range(2):
-        send(copy(wterm.at[7, n], prx.at[3, n], s_p.at[3, n], r_p.at[3, n], at(-1)))
+        send(copy(wterm.at[7, n], prx.at[3, n], s_p.at[0], r_p.at[0], at(-1)))
     for slot in (2, 1, 0):
         for n in range(2):
-            send(copy(wterm.at[2 * slot + 1, n], prx.at[slot, n], s_p.at[slot, n], r_p.at[slot, n], partner))
+            send(copy(wterm.at[2 * slot + 1, n], prx.at[slot, n], s_p.at[0], r_p.at[0], partner))
 
     gq = jnp.zeros((1, HD), F32)
     for g in range(G):
@@ -424,21 +439,20 @@
     grad = (dqt[:, ROWS:] * (tot[:, ROWS:] * SCALE)).T[0:16]
     raw, part = norm_back(grad, punit, pinverse, gain_q, pc16, ps16)
     gq = gq + part
-    row8 = lax.broadcasted_iota(jnp.int32, (8, HD), 0)
-    g1[z] = jnp.where(row8 == 0, gq, jnp.where(row8 == 1, gk, 0.0))
+    g1[z] = jnp.concatenate([gq, gk], axis=0)
     scr[...] = raw
     for g in range(G):
         pdq_ref[:, g * HD : (g + 1) * HD] = scr[2 * g : 2 * g + 2, :].astype(BF16)
 
     @pl.loop(1, Z)
     def _(j):
-        copy(g1.at[z], g1.at[z], s_g1.at[j], r_g1.at[z], z_dev(lax.rem(z + j, Z))).start()
-
-    def p_arrived(slot, n):
-        copy(prx.at[slot, n], prx.at[slot, n], s_p.at[slot, n], r_p.at[slot, n], partner).wait_recv()
+        copy(g1.at[z], g1.at[z], s_g1.at[0], r_g1.at[0], z_dev(lax.rem(z + j, Z))).start()
+
+    out = pltpu.make_async_copy(dq_ref, dq_hbm, s_loc.at[8])
+    out.start()
 
     def m_arrived(k, n):
-        copy(mrx.at[k, n], mrx.at[k, n], s_m.at[k, n], r_m.at[k, n], partner).wait_recv()
+        copy(mrx.at[k, n], mrx.at[k, n], s_m.at[0], r_m.at[k, n], partner).wait_recv()
 
     def step_down(k):
         for n in range(2):
@@ -451,16 +465,12 @@
                 value = value + mrx[k, n].astype(F32)
             mtx[k - 1, n] = value.astype(BF16)
         for n in range(2):
-            send(copy(mtx.at[k - 1, n], mrx.at[k - 1, n], s_m.at[k - 1, n], r_m.at[k - 1, n], at(-2)))
-
-    for slot in range(4):
-        for n in range(2):
-            p_arrived(slot, n)
+            send(copy(mtx.at[k - 1, n], mrx.at[k - 1, n], s_m.at[0], r_m.at[k - 1, n], at(-2)))
+
+    sum_wait(prx, 4, r_p.at[0])
     step_down(3)
 
-    for j in range(1, GRP):
-        slot = lax.rem(gi + j, GRP)
-        copy(rs1.at[slot], rs1.at[slot], s_rs1.at[j], r_rs1.at[slot], partner).wait_recv()
+    sum_wait(rs1, GRP - 1, r_rs1.at[0])
     rs1[gi] = pterm[gi]
     total = rs1[0].astype(F32)
     for n in range(1, GRP):
@@ -468,21 +478,17 @@
     dn[...] = total
     for n in range(2):
         for k in range(Z):
-            rs2t[k, n] = dn[n * 32 + 2 * k : n * 32 + 2 * k + 2, :]
+            rs2t[k, n] = dn[n * 32 + 2 * k : n * 32 + 2 * k + 2, :].astype(BF16)
     rs2[z] = rs2t[z]
 
     @pl.loop(1, Z)
     def _(j):
         other = lax.rem(z + j, Z)
-        copy(rs2t.at[other], rs2.at[z], s_rs2.at[j], r_rs2.at[z], z_dev(other)).start()
+        copy(rs2t.at[other], rs2.at[z], s_rs2.at[0], r_rs2.at[0], z_dev(other)).start()
 
     step_down(2)
 
-    @pl.loop(1, Z)
-    def _(j):
-        slot = lax.rem(z + j, Z)
-        copy(g1.at[slot], g1.at[slot], s_g1.at[j], r_g1.at[slot], partner).wait_recv()
-
+    sum_wait(g1, Z - 1, r_g1.at[0])
     total = g1[0]
     for n in range(1, Z):
         total = total + g1[n]
@@ -493,7 +499,7 @@
     def _(j):
         other = lax.rem(xg + j, GRP * X)
         copy(
-            g2.at[xg], g2.at[xg], s_g2.at[j], r_g2.at[xg], grp_dev(lax.rem(other, GRP)), other // GRP
+            g2.at[xg], g2.at[xg], s_g2.at[0], r_g2.at[0], grp_dev(lax.rem(other, GRP)), other // GRP
         ).start()
 
     step_down(1)
@@ -512,53 +518,43 @@
     dk_ref[...] = raw.astype(BF16)
     dv_ref[...] = ownv[...].astype(BF16)
 
-    @pl.loop(1, Z)
-    def _(j):
-        slot = lax.rem(z + j, Z)
-        copy(rs2.at[slot], rs2.at[slot], s_rs2.at[j], r_rs2.at[slot], partner).wait_recv()
-
-    ptk, ptv = rs2[0, 0], rs2[0, 1]
+    sum_wait(rs2, Z - 1, r_rs2.at[0])
+    ptk, ptv = rs2[0, 0].astype(F32), rs2[0, 1].astype(F32)
     for n in range(1, Z):
-        ptk = ptk + rs2[n, 0]
-        ptv = ptv + rs2[n, 1]
-    unit2, inverse2 = norm(pk_ref[...].astype(F32))
+        ptk = ptk + rs2[n, 0].astype(F32)
+        ptv = ptv + rs2[n, 1].astype(F32)
+    unit2, inverse2 = norm(zr[z, 0].astype(F32))
     raw, _ = norm_back(ptk, unit2, inverse2, gain_k, pc16[0:2], ps16[0:2])
     pdk_ref[...] = raw.astype(BF16)
     pdv_ref[...] = ptv.astype(BF16)
 
-    @pl.loop(1, GRP * X)
-    def _(j):
-        slot = lax.rem(xg + j, GRP * X)
-        copy(g2.at[slot], g2.at[slot], s_g2.at[j], r_g2.at[slot], partner).wait_recv()
-
+    sum_wait(g2, GRP * X - 1, r_g2.at[0])
     total = g2[0]
     for n in range(1, GRP * X):
         total = total + g2[n]
     count = (NCTX * (BLK + 2)) * X
-    factor = jnp.where(row8 == 0, (count * G) ** (-0.5), count ** (-0.5))
-    gg_ref[...] = (total * factor)[0:2]
-
-    for cp in sent:
-        cp.wait_send()
-
-    @pl.when(c == 0)
-    def _():
-        for n in range(2):
-            kv_copy(1, n, 0, 1, partner).wait_send()
-
-    @pl.when(c == 1)
-    def _():
-        for n in range(2):
-            kv_copy(7, n, 6, 5, partner).wait_send()
-
-    @pl.loop(1, Z)
-    def _(j):
-        copy(rs2t.at[z], rs2.at[z], s_rs2.at[j], r_rs2.at[z], partner).wait_send()
-        copy(g1.at[z], g1.at[z], s_g1.at[j], r_g1.at[z], partner).wait_send()
-
-    @pl.loop(1, GRP * X)
-    def _(j):
-        copy(g2.at[0], g2.at[0], s_g2.at[j], r_g2.at[0], partner).wait_send()
+    row2 = lax.broadcasted_iota(jnp.int32, (2, HD), 0)
+    factor = jnp.where(row2 == 0, (count * G) ** (-0.5), count ** (-0.5))
+    gg_ref[...] = total * factor
+
+    out.wait()
+    sent(zr, 4 * JUMP - 1, s_zr.at[0])
+    sent(parw, SUB - 1, s_par.at[0])
+    sent(kv, 7, s_kv.at[0])
+    for n in range(2):
+        sent(grp.at[n], GRP - 1, s_ag2.at[n])
+    sent(rs1, GRP - 1, s_rs1.at[0])
+    sent(prx, 4, s_p.at[0])
+    sent(mrx, 3, s_m.at[0])
+    sent(rs2, Z - 1, s_rs2.at[0])
+    sent(g1, Z - 1, s_g1.at[0])
+    sent(g2, GRP * X - 1, s_g2.at[0])
+
+
+def finish(*refs):
+    count = len(refs) // 2
+    for src, dst in zip(refs[:count], refs[count:]):
+        dst[...] = src[...]
 
 
 def per_device(
@@ -568,7 +564,6 @@
     offset, level, prompt = tables()
     vmem = pl.BlockSpec(memory_space=pltpu.VMEM)
     hbm = pl.BlockSpec(memory_space=pl.ANY)
-    smem = pl.BlockSpec(memory_space=pltpu.SMEM)
     dma = pltpu.SemaphoreType.DMA
     vm = pltpu.VMEM
     outs = pl.pallas_call(
@@ -582,18 +577,20 @@
             jax.ShapeDtypeStruct((2, HD), BF16),
             jax.ShapeDtypeStruct((2, HD), F32),
         ),
-        in_specs=[hbm] * 5 + [vmem] * 6 + [smem, vmem, hbm, vmem, hbm],
-        out_specs=(vmem,) * 7,
+        in_specs=[hbm] * 14,
+        out_specs=(hbm,) + (vmem,) * 6,
         scratch_shapes=[
+            vm((3, BLK, G * HD), BF16),
+            vm((3, 2, G * HD), BF16),
+            vm((2, BLK + 16 + PFX, HD), F32),
             vm((BLK, G * HD), BF16),
-            vm((BLK, G * HD), BF16),
-            vm((BLK, G * HD), BF16),
-            vm((2, BLK, HD), F32),
-            vm((2, PFX, HD), F32),
+            vm((2, HD), F32),
+            vm((1, 1), jnp.int32),
+            vm((1, HD), jnp.int32),
             vm((SUB, 2, BLK, HD), BF16),
             vm((SUB, 1, HD), jnp.int32),
             vm((Z, 2, 2, HD), BF16),
-            vm((GRP, 64, HD), BF16),
+            vm((2, GRP, 32, HD), BF16),
             vm((ALLR, HD), BF16),
             vm((ROWS, HD), F32),
             vm((ROWS, HD), F32),
@@ -615,7 +612,6 @@
             vm((16, HD), F32),
             vm((PROWS, HD), F32),
             vm((64, HD), F32),
-            vm((PFX, HD), BF16),
             vm((SUB, 2, BLK, HD), BF16),
             vm((BLK, HD), F32),
             vm((BLK, HD), F32),
@@ -624,21 +620,21 @@
             vm((3, 2, BLK, HD), BF16),
             vm((GRP, 64, HD), BF16),
             vm((GRP, 64, HD), BF16),
-            vm((Z, 2, 2, HD), F32),
-            vm((Z, 2, 2, HD), F32),
-            vm((Z, 8, HD), F32),
-            vm((GRP * X, 8, HD), F32),
-            dma((7,)),
-            dma((8, 2)), dma((SUB, 2)),
-            dma((SUB,)), dma((SUB,)),
-            dma((4 * JUMP + 1,)), dma((Z,)),
-            dma((GRP,)), dma((GRP,)),
-            dma((4, 2)), dma((4, 2)),
-            dma((3, 2)), dma((3, 2)),
-            dma((GRP,)), dma((GRP,)),
-            dma((Z,)), dma((Z,)),
-            dma((Z,)), dma((Z,)),
-            dma((GRP * X,)), dma((GRP * X,)),
+            vm((Z, 2, 2, HD), BF16),
+            vm((Z, 2, 2, HD), BF16),
+            vm((Z, 2, HD), F32),
+            vm((GRP * X, 2, HD), F32),
+            dma((9,)),
+            dma((1,)), dma((SUB, 2)),
+            dma((1,)), dma((1,)),
+            dma((1,)), dma((2,)),
+            dma((2,)), dma((2,)),
+            dma((1,)), dma((1,)),
+            dma((1,)), dma((3, 2)),
+            dma((1,)), dma((1,)),
+            dma((1,)), dma((1,)),
+            dma((1,)), dma((1,)),
+            dma((1,)), dma((1,)),
         ],
         compiler_params=pltpu.CompilerParams(
             collective_id=0, has_side_effects=True, vmem_limit_bytes=60 * 1024 * 1024
@@ -647,9 +643,16 @@
     )(
         branch_q[:, 0], branch_k[:, 0], branch_v[:, 0], branch_o[:, 0], branch_dout[:, 0],
         prompt_q[:, 0], prompt_k[:, 0], prompt_v[:, 0], prompt_o[:, 0], prompt_dout[:, 0],
-        gains, parents, depth.reshape(1, BLK),
-        jnp.asarray(offset), jnp.asarray(level), jnp.asarray(prompt),
+        gains, parents.reshape(1, 1), depth.reshape(1, BLK),
+        jnp.asarray(np.concatenate([offset, level, prompt], axis=1)),
     )
+    outs = pl.pallas_call(
+        finish,
+        out_shape=tuple(jax.ShapeDtypeStruct(x.shape, x.dtype) for x in outs),
+        in_specs=[vmem] * 7,
+        out_specs=(vmem,) * 7,
+        name="finish",
+    )(*outs)
     dq, dk, dv, pdq, pdk, pdv, gain_grads = outs
     return (
         dq[:, None], dk[:, None], dv[:, None], pdq[:, None], pdk[:, None], pdv[:, None], gain_grads,

time: 59.8 us -> 49.7 us (0.83)
  local copies, waits for them, and re-layouts: 5.67 us -> 0 us
  Pallas kernels: 52.5 us -> 48.2 us
    pallas_call x1, Pallas kernels: 52.5 us -> 46.5 us  [per_device(): pl.pallas_call(kernel, out_shape=(jax.ShapeDtypeStruct((BLK, G * HD), BF1...]
    unnamed x19 -> x0, local copies, waits for them, and re-layouts: 5.67 us -> none
    pallas_call x0 -> x1, Pallas kernels: none -> 1.72 us  [per_device(): pl.pallas_call(finish, out_shape=tuple((jax.ShapeDtypeStruct(x.shape, x.d...]
where the time goes in v3:
time: 49.7 us; the launch traced here: 49.5 us
  Pallas kernels  48.2 us (97%)
  between operations  1.29 us (3%)
    pallas_call x1, Pallas kernels, per_device(): pl.pallas_call(kernel, out_shape=(jax.ShapeDtypeStruct((BLK, G * HD), BF1...  46.5 us
    pallas_call x1, Pallas kernels, per_device(): pl.pallas_call(finish, out_shape=tuple((jax.ShapeDtypeStruct(x.shape, x.d...  1.72 us

profile of v3, /device:TPU:1, one launch (start us, length us, event | category | flops | bytes accessed | tf_op | source)
XLA Modules:
  0.0 49.5 jit_solution(5306659831310134884)
XLA Ops:
  1.3 46.5 %tree_back.1 = (bf16[128,1024]{1,0:T(8,128)(2,1)}, bf16[128,128]{1,0:T(8,128)(2,1)}, bf16[128,128]{1,0:T(8,128)(2,1)}, bf16[2,1024]{1,0:T(2,128)(2,1)}, bf16[2,1...) custom-call(bf16[128,1024]{1,0:T(8,128)(2,1)} %bitcast.19, bf16[128,128]{1,0:T(8,128)(2,1)} %bitcast.22, ...), custom_call_target="tpu_custom_call" | custom-call | tf_op jit(solution)/shard_map/tree_back/pallas_call | solution.py:569
  47.8 1.7 %finish.1 = (bf16[128,1024]{1,0:T(8,128)(2,1)}, bf16[128,128]{1,0:T(8,128)(2,1)}, bf16[128,128]{1,0:T(8,128)(2,1)}, bf16[2,1024]{1,0:T(2,128)(2,1)}, bf16[2,128]...) custom-call(bf16[128,1024]{1,0:T(8,128)(2,1)} %get-tuple-element.21.refs_0_, ...), custom_call_target="tpu_custom_call" | custom-call | tf_op jit(solution)/shard_map/finish/pallas_call | solution.py:649

commit v4 on v3

--- a/solution.py
+++ b/solution.py
@@ -345,28 +345,28 @@
     kv_arrived(1)
     window(1, 2)
 
-    def last_hop(n):
-        kv_arrived(6, (n,))
-        send(kv_copy(n, 6, 7, at(1)))
-
-        @pl.when(c == 1)
-        def _():
-            kv_copy(n, 6, 5, partner).start()
-
-    for n in range(2):
-        last_hop(n)
-
     sum_wait(zr, 2 * JUMP - 1, r_zr.at[1])
     for n in range(2):
         for k in range(Z):
             dn[n * 32 + 2 * k : n * 32 + 2 * k + 2, :] = zr[k, n].astype(F32)
     grp[0, gi] = dn[0:32, :].astype(BF16)
     grp[1, gi] = dn[32:64, :].astype(BF16)
-    kv_arrived(3)
     for n in range(2):
         for j in range(1, GRP):
             other = grp_dev(lax.rem(gi + j, GRP))
             send(copy(grp.at[n, gi], grp.at[n, gi], s_ag2.at[n], r_ag2.at[n], other))
+    def last_hop(n):
+        kv_arrived(6, (n,))
+        send(kv_copy(n, 6, 7, at(1)))
+
+        @pl.when(c == 1)
+        def _():
+            kv_copy(n, 6, 5, partner).start()
+
+    for n in range(2):
+        last_hop(n)
+
+    kv_arrived(3)
     window(3, 2)
     kv_arrived(5)
     kv_arrived(7)
@@ -412,22 +412,32 @@
         other = lax.rem(gi + j, GRP)
         send(copy(pterm.at[other], rs1.at[gi], s_rs1.at[0], r_rs1.at[0], grp_dev(other)))
 
-    dk, dv = key_grads(slice(PFX, KEYS), ROWS)
-    for d in range(SUB - 1, -1, -1):
-        rows = slice(d * BLK, (d + 1) * BLK)
-        if d:
-            wterm[d, 0] = dk[rows].astype(BF16)
-            wterm[d, 1] = dv[rows].astype(BF16)
-        else:
-            ownk[...] = dk[rows]
-            ownv[...] = dv[rows]
-        g_part = unrotate(dk[rows], ctab[d], stab[d]) * kunit[PFX + d * BLK : PFX + (d + 1) * BLK, :]
-        gk = gk + jnp.sum(g_part, axis=0, keepdims=True)
-    for n in range(2):
-        send(copy(wterm.at[7, n], prx.at[3, n], s_p.at[0], r_p.at[0], at(-1)))
-    for slot in (2, 1, 0):
+    def window_grads(first, last):
+        dk, dv = key_grads(slice(PFX + first * BLK, PFX + (last + 1) * BLK), ROWS)
+        part = jnp.zeros((1, HD), F32)
+        for d in range(last, first - 1, -1):
+            rows = slice((d - first) * BLK, (d - first + 1) * BLK)
+            if d:
+                wterm[d, 0] = dk[rows].astype(BF16)
+                wterm[d, 1] = dv[rows].astype(BF16)
+            else:
+                ownk[...] = dk[rows]
+                ownv[...] = dv[rows]
+            keys = slice(PFX + d * BLK, PFX + (d + 1) * BLK)
+            part = part + jnp.sum(unrotate(dk[rows], ctab[d], stab[d]) * kunit[keys, :], axis=0, keepdims=True)
+        return part
+
+    def term_out(slot):
         for n in range(2):
-            send(copy(wterm.at[2 * slot + 1, n], prx.at[slot, n], s_p.at[0], r_p.at[0], partner))
+            device = partner if slot < 3 else at(-1)
+            send(copy(wterm.at[2 * slot + 1, n], prx.at[slot, n], s_p.at[0], r_p.at[slot // 2], device))
+
+    gk = gk + window_grads(5, 7)
+    term_out(3)
+    term_out(2)
+    gk = gk + window_grads(0, 4)
+    term_out(1)
+    term_out(0)
 
     gq = jnp.zeros((1, HD), F32)
     for g in range(G):
@@ -464,11 +474,11 @@
             else:
                 value = value + mrx[k, n].astype(F32)
             mtx[k - 1, n] = value.astype(BF16)
-        for n in range(2):
             send(copy(mtx.at[k - 1, n], mrx.at[k - 1, n], s_m.at[0], r_m.at[k - 1, n], at(-2)))
 
-    sum_wait(prx, 4, r_p.at[0])
+    sum_wait(prx, 2, r_p.at[1])
     step_down(3)
+    sum_wait(prx, 2, r_p.at[0])
 
     sum_wait(rs1, GRP - 1, r_rs1.at[0])
     rs1[gi] = pterm[gi]
@@ -629,7 +639,7 @@
             dma((1,)), dma((1,)),
             dma((1,)), dma((2,)),
             dma((2,)), dma((2,)),
-            dma((1,)), dma((1,)),
+            dma((1,)), dma((2,)),
             dma((1,)), dma((3, 2)),
             dma((1,)), dma((1,)),
             dma((1,)), dma((1,)),

time: 49.7 us -> 48.7 us (0.980)
  Pallas kernels: 48.2 us -> 47.3 us
    pallas_call x1, Pallas kernels: 46.5 us -> 45.6 us  [per_device(): pl.pallas_call(kernel, out_shape=(jax.ShapeDtypeStruct((BLK, G * HD), BF1...]
where the time goes in v4:
time: 48.7 us; the launch traced here: 48.6 us
  Pallas kernels  47.3 us (97%)
  between operations  1.29 us (3%)
    pallas_call x1, Pallas kernels, per_device(): pl.pallas_call(kernel, out_shape=(jax.ShapeDtypeStruct((BLK, G * HD), BF1...  45.6 us
    pallas_call x1, Pallas kernels, per_device(): pl.pallas_call(finish, out_shape=tuple((jax.ShapeDtypeStruct(x.shape, x.d...  1.72 us

profile of v4, /device:TPU:1, one launch (start us, length us, event | category | flops | bytes accessed | tf_op | source)
XLA Modules:
  0.0 48.6 jit_solution(6168142820810797860)
XLA Ops:
  1.3 45.6 %tree_back.1 = (bf16[128,1024]{1,0:T(8,128)(2,1)}, bf16[128,128]{1,0:T(8,128)(2,1)}, bf16[128,128]{1,0:T(8,128)(2,1)}, bf16[2,1024]{1,0:T(2,128)(2,1)}, bf16[2,1...) custom-call(bf16[128,1024]{1,0:T(8,128)(2,1)} %bitcast.19, bf16[128,128]{1,0:T(8,128)(2,1)} %bitcast.22, ...), custom_call_target="tpu_custom_call" | custom-call | tf_op jit(solution)/shard_map/tree_back/pallas_call | solution.py:579
  46.8 1.7 %finish.1 = (bf16[128,1024]{1,0:T(8,128)(2,1)}, bf16[128,128]{1,0:T(8,128)(2,1)}, bf16[128,128]{1,0:T(8,128)(2,1)}, bf16[2,1024]{1,0:T(2,128)(2,1)}, bf16[2,128]...) custom-call(bf16[128,1024]{1,0:T(8,128)(2,1)} %get-tuple-element.21.refs_0_, ...), custom_call_target="tpu_custom_call" | custom-call | tf_op jit(solution)/shard_map/finish/pallas_call | solution.py:659

commit v5 on v4

--- a/solution.py
+++ b/solution.py
@@ -252,32 +252,6 @@
         if j < JUMP:
             zr_send(1, z_at(j), z_at(-JUMP))
 
-    def to_rows(n):
-        x = pqod[n].astype(F32)
-        for g in range(G):
-            scr[2 * g : 2 * g + 2, :] = x[:, g * HD : (g + 1) * HD]
-        return scr[0:16, :]
-
-    pslot = gi * 32 + z * 2
-    odd = lax.rem(row16, 2) == 1
-
-    def prow(n):
-        first = jnp.broadcast_to(tpr_ref[n, pl.ds(pslot, 1), :], (16, HD))
-        second = jnp.broadcast_to(tpr_ref[n, pl.ds(pslot + 1, 1), :], (16, HD))
-        return jnp.where(odd, second, first)
-
-    pc16, ps16 = prow(0), prow(1)
-    prest = pl.ds(ROWS + 16, PROWS - 16)
-    punit, pinverse = norm(to_rows(0))
-    qrot[ROWS : ROWS + 16, :] = rotate(punit * gain_q, pc16, ps16).astype(BF16)
-    qrot[prest, :] = jnp.zeros((PROWS - 16, HD), BF16)
-    pd = to_rows(2)
-    dor[ROWS : ROWS + 16, :] = pd.astype(BF16)
-    dor[prest, :] = jnp.zeros((PROWS - 16, HD), BF16)
-    pscr[...] = jnp.zeros((PROWS, HD), F32)
-    pscr[0:16, :] = pd * to_rows(1)
-    delta[:, ROWS:] = jnp.sum(pscr[...].T, axis=0, keepdims=True)
-
     tot[...] = jnp.zeros((1, ALLR), F32)
     dqt[...] = jnp.zeros((HD, ALLR), F32)
 
@@ -371,6 +345,32 @@
     kv_arrived(5)
     kv_arrived(7)
     window(5, 3)
+
+    def to_rows(n):
+        x = pqod[n].astype(F32)
+        for g in range(G):
+            scr[2 * g : 2 * g + 2, :] = x[:, g * HD : (g + 1) * HD]
+        return scr[0:16, :]
+
+    pslot = gi * 32 + z * 2
+    odd = lax.rem(row16, 2) == 1
+
+    def prow(n):
+        first = jnp.broadcast_to(tpr_ref[n, pl.ds(pslot, 1), :], (16, HD))
+        second = jnp.broadcast_to(tpr_ref[n, pl.ds(pslot + 1, 1), :], (16, HD))
+        return jnp.where(odd, second, first)
+
+    pc16, ps16 = prow(0), prow(1)
+    prest = pl.ds(ROWS + 16, PROWS - 16)
+    punit, pinverse = norm(to_rows(0))
+    qrot[ROWS : ROWS + 16, :] = rotate(punit * gain_q, pc16, ps16).astype(BF16)
+    qrot[prest, :] = jnp.zeros((PROWS - 16, HD), BF16)
+    pd = to_rows(2)
+    dor[ROWS : ROWS + 16, :] = pd.astype(BF16)
+    dor[prest, :] = jnp.zeros((PROWS - 16, HD), BF16)
+    pscr[...] = jnp.zeros((PROWS, HD), F32)
+    pscr[0:16, :] = pd * to_rows(1)
+    delta[:, ROWS:] = jnp.sum(pscr[...].T, axis=0, keepdims=True)
 
     def grp_arrived(n):
         sum_wait(grp.at[n], GRP - 1, r_ag2.at[n])

time: 48.7 us -> 48.7 us (level)
  no operation moved by 1% of the time
where the time goes in v5:
time: 48.7 us; the launch traced here: 48.6 us
  Pallas kernels  47.3 us (97%)
  between operations  1.29 us (3%)
    pallas_call x1, Pallas kernels, per_device(): pl.pallas_call(kernel, out_shape=(jax.ShapeDtypeStruct((BLK, G * HD), BF1...  45.6 us
    pallas_call x1, Pallas kernels, per_device(): pl.pallas_call(finish, out_shape=tuple((jax.ShapeDtypeStruct(x.shape, x.d...  1.72 us

profile of v5, /device:TPU:1, one launch (start us, length us, event | category | flops | bytes accessed | tf_op | source)
XLA Modules:
  0.0 48.6 jit_solution(17988571107746407196)
XLA Ops:
  1.3 45.6 %tree_back.1 = (bf16[128,1024]{1,0:T(8,128)(2,1)}, bf16[128,128]{1,0:T(8,128)(2,1)}, bf16[128,128]{1,0:T(8,128)(2,1)}, bf16[2,1024]{1,0:T(2,128)(2,1)}, bf16[2,1...) custom-call(bf16[128,1024]{1,0:T(8,128)(2,1)} %bitcast.19, bf16[128,128]{1,0:T(8,128)(2,1)} %bitcast.22, ...), custom_call_target="tpu_custom_call" | custom-call | tf_op jit(solution)/shard_map/tree_back/pallas_call | solution.py:579
  46.9 1.7 %finish.1 = (bf16[128,1024]{1,0:T(8,128)(2,1)}, bf16[128,128]{1,0:T(8,128)(2,1)}, bf16[128,128]{1,0:T(8,128)(2,1)}, bf16[2,1024]{1,0:T(2,128)(2,1)}, bf16[2,128]...) custom-call(bf16[128,1024]{1,0:T(8,128)(2,1)} %get-tuple-element.21.refs_0_, ...), custom_call_target="tpu_custom_call" | custom-call | tf_op jit(solution)/shard_map/finish/pallas_call | solution.py:659
